TPU v7x, 32 devices: a whole 2x2x4 slice. The times are simulated.
32 devices in a mesh: dp: 8 (over y, x, core), mem: 4 (over z).
Axes of the slice: x: 2, y: 2, z: 4, core: 2. Of those that a mesh axis runs over, the one named last changes fastest.
Arguments:
- inputs: bfloat16 [32, 100, 768], P('dp'), may hold values from -6 to 6
- memory: bfloat16 [32, 1280, 768], P('dp', 'mem'), may hold values from -6 to 6
- lengths: int32 [32], P('dp'), may hold values from 1 to 1280, as said below
- self_query: bfloat16 [768, 768], P('dp'), may hold values from -0.21875 to 0.21875
- self_key: bfloat16 [768, 768], P('dp'), may hold values from -0.21875 to 0.21875
- self_value: bfloat16 [768, 768], P('dp'), may hold values from -0.21875 to 0.21875
- self_out: bfloat16 [768, 768], P('dp'), may hold values from -0.625 to 0.625
- cross_query: bfloat16 [768, 768], P('dp'), may hold values from -0.21875 to 0.21875
- cross_key: bfloat16 [768, 768], P('dp'), may hold values from -0.21875 to 0.21875
- cross_value: bfloat16 [768, 768], P('dp'), may hold values from -0.21875 to 0.21875
- cross_out: bfloat16 [768, 768], P('dp'), may hold values from -1 to 1
- expand_weight: bfloat16 [768, 3072], P('dp'), may hold values from -0.21875 to 0.21875
- contract_weight: bfloat16 [3072, 768], P('dp'), may hold values from -0.109375 to 0.109375
- gain_one: float32 [768], replicated, may hold values from 0.5 to 1.5
- shift_one: float32 [768], replicated, may hold values from -1.5 to 1.5
- gain_two: float32 [768], replicated, may hold values from 0.5 to 1.5
- shift_two: float32 [768], replicated, may hold values from -1.5 to 1.5
- gain_three: float32 [768], replicated, may hold values from 0.5 to 1.5
- shift_three: float32 [768], replicated, may hold values from -1.5 to 1.5
- cotangent: bfloat16 [32, 100, 768], P('dp'), may hold values from -6 to 6
Outputs:
- output: float32 [32, 100, 768], P('dp')
- input_grad: float32 [32, 100, 768], P('dp')
- memory_grad: float32 [32, 1280, 768], P('dp', 'mem')
- self_query_grad: float32 [768, 768], P('dp')
- self_key_grad: float32 [768, 768], P('dp')
- self_value_grad: float32 [768, 768], P('dp')
- self_out_grad: float32 [768, 768], P('dp')
- cross_query_grad: float32 [768, 768], P('dp')
- cross_key_grad: float32 [768, 768], P(('dp', 'mem'))
- cross_value_grad: float32 [768, 768], P(('dp', 'mem'))
- cross_out_grad: float32 [768, 768], P('dp')
- expand_grad: float32 [768, 3072], P('dp')
- contract_grad: float32 [3072, 768], P('dp')
- gain_one_grad: float32 [768], P('dp')
- shift_one_grad: float32 [768], P('dp')
- gain_two_grad: float32 [768], P('dp')
- shift_two_grad: float32 [768], P('dp')
- gain_three_grad: float32 [768], P('dp')
- shift_three_grad: float32 [768], P('dp')
Inputs may be any that keep to these rules, and one draw needn't show every extreme that they name: `lengths`: the number of valid memory tokens of each image; in each aligned block of 4 images one image has all 1280.
All inputs are finite; a program needn't handle non-finite values.
Results may differ from a plain program's by a relative error of at most 0.023.
Values may be sent and summed in bfloat16 or wider, within the bound.
A program may use at most 320 MiB of HBM per device.

v0:
```python
import jax
import jax.numpy as jnp
from jax import lax
from jax.sharding import PartitionSpec as P

H = 12
MICRO = 4


def project(values, weight):
    return jnp.einsum("btd,df->btf", values, weight, preferred_element_type=jnp.float32)


def back_project(grads, weight):
    return jnp.einsum("btf,df->btd", grads, weight, preferred_element_type=jnp.float32)


def weight_grad(left, right):
    return jnp.einsum("btd,btf->df", left, right, preferred_element_type=jnp.float32)


def split_heads(values):
    layout = values.shape
    return values.reshape(layout[0], layout[1], H, layout[2] // H).transpose(0, 2, 1, 3)


def join_heads(values):
    layout = values.shape
    return values.transpose(0, 2, 1, 3).reshape(layout[0], layout[2], layout[1] * layout[3])


def head_scores(query, keys):
    return jnp.einsum("bhqe,bhke->bhqk", query, keys, preferred_element_type=jnp.float32) * 0.125


def norm_forward(resid, gain, shift):
    center = resid - jnp.mean(resid, axis=-1, keepdims=True)
    inverse = lax.rsqrt(jnp.mean(center * center, axis=-1, keepdims=True) + 1e-05)
    normed = center * inverse
    return (normed * gain + shift, normed, inverse)


def norm_backward(incoming, normed, inverse, gain):
    scaled = incoming * gain
    grad_in = inverse * (
        scaled
        - jnp.mean(scaled, axis=-1, keepdims=True)
        - normed * jnp.mean(scaled * normed, axis=-1, keepdims=True)
    )
    return (grad_in, jnp.sum(incoming * normed, axis=(0, 1)), jnp.sum(incoming, axis=(0, 1)))


def score_grads(probs, grad_probs, row_term, query, keys):
    grad_scores = (probs * (grad_probs - row_term)).astype(jnp.bfloat16)
    grad_query = (
        jnp.einsum("bhqk,bhke->bhqe", grad_scores, keys, preferred_element_type=jnp.float32) * 0.125
    )
    grad_keys = (
        jnp.einsum("bhqk,bhqe->bhke", grad_scores, query, preferred_element_type=jnp.float32)
        * 0.125
    )
    return (grad_query, grad_keys)


def value_grads(probs, grad_heads):
    return jnp.einsum(
        "bhqk,bhqe->bhke",
        probs.astype(jnp.bfloat16),
        grad_heads,
        preferred_element_type=jnp.float32,
    )


def gelu_tanh(values):
    return jax.nn.gelu(values, approximate=True)


def on_device(
    inputs,
    memory,
    lengths,
    self_query,
    self_key,
    self_value,
    self_out,
    cross_query,
    cross_key,
    cross_value,
    cross_out,
    expand_weight,
    contract_weight,
    gain_one,
    shift_one,
    gain_two,
    shift_two,
    gain_three,
    shift_three,
    cotangent,
):
    low_type = jnp.bfloat16
    per_batch = inputs.shape[0] // MICRO
    mem_rows = memory.shape[1]
    key_places = lax.axis_index("mem") * mem_rows + jnp.arange(mem_rows, dtype=jnp.int32)
    outputs = []
    input_grads = []
    memory_grads = []
    summed = None
    kv_summed = None
    gathered = None
    for micro_step in range(MICRO):
        gathered = (
            lax.all_gather(self_query, "dp", axis=0, tiled=True),
            lax.all_gather(self_key, "dp", axis=0, tiled=True),
            lax.all_gather(self_value, "dp", axis=0, tiled=True),
            lax.all_gather(self_out, "dp", axis=0, tiled=True),
            lax.all_gather(cross_query, "dp", axis=0, tiled=True),
            lax.all_gather(cross_key, "dp", axis=0, tiled=True),
            lax.all_gather(cross_value, "dp", axis=0, tiled=True),
            lax.all_gather(cross_out, "dp", axis=0, tiled=True),
            lax.all_gather(expand_weight, "dp", axis=0, tiled=True),
            lax.all_gather(contract_weight, "dp", axis=0, tiled=True),
        )
        (
            query_full,
            key_full,
            value_full,
            out_full,
            cquery_full,
            ckey_full,
            cvalue_full,
            cout_full,
            expand_full,
            contract_full,
        ) = gathered
        begin = micro_step * per_batch
        finish = begin + per_batch
        tokens = inputs[begin:finish]
        memory_part = memory[begin:finish]
        length_part = lengths[begin:finish]
        incoming = cotangent[begin:finish].astype(jnp.float32)
        query_heads = split_heads(project(tokens, query_full).astype(low_type))
        key_heads = split_heads(project(tokens, key_full).astype(low_type))
        value_heads = split_heads(project(tokens, value_full).astype(low_type))
        self_raw = head_scores(query_heads, key_heads)
        self_top = jnp.max(self_raw, axis=-1, keepdims=True)
        self_denom = jnp.sum(jnp.exp(self_raw - self_top), axis=-1, keepdims=True)
        self_probs = jnp.exp(self_raw - self_top) / self_denom
        self_attn = join_heads(
            jnp.einsum(
                "bhqk,bhke->bhqe",
                self_probs.astype(low_type),
                value_heads,
                preferred_element_type=jnp.float32,
            )
        ).astype(low_type)
        self_branch = project(self_attn, out_full)
        first, normed_one, inverse_one = norm_forward(
            tokens.astype(jnp.float32) + self_branch, gain_one, shift_one
        )
        first_low = first.astype(low_type)
        cross_q = split_heads(project(first_low, cquery_full).astype(low_type))
        cross_k = split_heads(project(memory_part, ckey_full).astype(low_type))
        cross_v = split_heads(project(memory_part, cvalue_full).astype(low_type))
        valid = (key_places[None, :] < length_part[:, None])[:, None, None, :]
        cross_raw = jnp.where(valid, head_scores(cross_q, cross_k), -1e30)
        local_top = jnp.max(cross_raw, axis=-1, keepdims=True)
        global_top = lax.pmax(local_top, "mem")
        global_sum = lax.psum(
            jnp.sum(jnp.where(valid, jnp.exp(cross_raw - global_top), 0.0), axis=-1, keepdims=True),
            "mem",
        )
        cross_probs = jnp.where(valid, jnp.exp(cross_raw - global_top), 0.0) / global_sum
        partial_numer = join_heads(
            jnp.einsum(
                "bhqk,bhke->bhqe",
                cross_probs.astype(low_type),
                cross_v,
                preferred_element_type=jnp.float32,
            )
        )
        cross_attn = (
            lax.psum(partial_numer.astype(jnp.bfloat16), "mem").astype(jnp.float32).astype(low_type)
        )
        cross_branch = project(cross_attn, cout_full)
        second, normed_two, inverse_two = norm_forward(first + cross_branch, gain_two, shift_two)
        second_low = second.astype(low_type)
        pre_act = project(second_low, expand_full)
        activ, gelu_pull = jax.vjp(gelu_tanh, pre_act)
        activ_low = activ.astype(low_type)
        ffn_branch = project(activ_low, contract_full)
        result, normed_three, inverse_three = norm_forward(
            second + ffn_branch, gain_three, shift_three
        )
        outputs.append(result)
        grad_three, gain_three_part, shift_three_part = norm_backward(
            incoming, normed_three, inverse_three, gain_three
        )
        grad_ffn = grad_three.astype(low_type)
        contract_part = weight_grad(activ_low, grad_ffn)
        grad_pre = gelu_pull(back_project(grad_ffn, contract_full))[0].astype(low_type)
        expand_part = weight_grad(second_low, grad_pre)
        grad_second = grad_three + back_project(grad_pre, expand_full)
        grad_two, gain_two_part, shift_two_part = norm_backward(
            grad_second, normed_two, inverse_two, gain_two
        )
        grad_cross = grad_two.astype(low_type)
        cout_part = weight_grad(cross_attn, grad_cross)
        grad_cattn = split_heads(back_project(grad_cross, cout_full).astype(low_type))
        again_raw = jnp.where(valid, head_scores(cross_q, cross_k), -1e30)
        again_probs = jnp.where(valid, jnp.exp(again_raw - global_top), 0.0) / global_sum
        cross_grad_probs = jnp.einsum(
            "bhqe,bhke->bhqk", grad_cattn, cross_v, preferred_element_type=jnp.float32
        )
        cross_row = lax.psum(jnp.sum(again_probs * cross_grad_probs, axis=-1, keepdims=True), "mem")
        part_cquery, grad_ckey_heads = score_grads(
            again_probs, cross_grad_probs, cross_row, cross_q, cross_k
        )
        grad_cquery = (
            lax.psum(join_heads(part_cquery).astype(jnp.bfloat16), "mem")
            .astype(jnp.float32)
            .astype(low_type)
        )
        grad_ckey = join_heads(grad_ckey_heads).astype(low_type)
        grad_cvalue = join_heads(value_grads(again_probs, grad_cattn)).astype(low_type)
        cquery_part = weight_grad(first_low, grad_cquery)
        ckey_part = weight_grad(memory_part, grad_ckey)
        cvalue_part = weight_grad(memory_part, grad_cvalue)
        memory_grads.append(
            back_project(grad_ckey, ckey_full) + back_project(grad_cvalue, cvalue_full)
        )
        grad_first = grad_two + back_project(grad_cquery, cquery_full)
        grad_one, gain_one_part, shift_one_part = norm_backward(
            grad_first, normed_one, inverse_one, gain_one
        )
        grad_self = grad_one.astype(low_type)
        out_part = weight_grad(self_attn, grad_self)
        grad_sattn = split_heads(back_project(grad_self, out_full).astype(low_type))
        again_self = head_scores(query_heads, key_heads)
        again_sprobs = jnp.exp(again_self - self_top) / self_denom
        self_grad_probs = jnp.einsum(
            "bhqe,bhke->bhqk", grad_sattn, value_heads, preferred_element_type=jnp.float32
        )
        self_row = jnp.sum(again_sprobs * self_grad_probs, axis=-1, keepdims=True)
        grad_query_heads, grad_key_heads = score_grads(
            again_sprobs, self_grad_probs, self_row, query_heads, key_heads
        )
        grad_query = join_heads(grad_query_heads).astype(low_type)
        grad_key = join_heads(grad_key_heads).astype(low_type)
        grad_value = join_heads(value_grads(again_sprobs, grad_sattn)).astype(low_type)
        query_part = weight_grad(tokens, grad_query)
        key_part = weight_grad(tokens, grad_key)
        value_part = weight_grad(tokens, grad_value)
        input_grads.append(
            grad_one
            + back_project(grad_query, query_full)
            + back_project(grad_key, key_full)
            + back_project(grad_value, value_full)
        )
        shard_parts = (
            lax.psum_scatter(
                query_part.astype(jnp.bfloat16), "dp", scatter_dimension=0, tiled=True
            ).astype(jnp.float32),
            lax.psum_scatter(
                key_part.astype(jnp.bfloat16), "dp", scatter_dimension=0, tiled=True
            ).astype(jnp.float32),
            lax.psum_scatter(
                value_part.astype(jnp.bfloat16), "dp", scatter_dimension=0, tiled=True
            ).astype(jnp.float32),
            lax.psum_scatter(
                out_part.astype(jnp.bfloat16), "dp", scatter_dimension=0, tiled=True
            ).astype(jnp.float32),
            lax.psum_scatter(
                cquery_part.astype(jnp.bfloat16), "dp", scatter_dimension=0, tiled=True
            ).astype(jnp.float32),
            lax.psum_scatter(
                cout_part.astype(jnp.bfloat16), "dp", scatter_dimension=0, tiled=True
            ).astype(jnp.float32),
            lax.psum_scatter(
                expand_part.astype(jnp.bfloat16), "dp", scatter_dimension=0, tiled=True
            ).astype(jnp.float32),
            lax.psum_scatter(
                contract_part.astype(jnp.bfloat16), "dp", scatter_dimension=0, tiled=True
            ).astype(jnp.float32),
            lax.psum_scatter(
                gain_one_part.astype(jnp.bfloat16), "dp", scatter_dimension=0, tiled=True
            ).astype(jnp.float32),
            lax.psum_scatter(
                shift_one_part.astype(jnp.bfloat16), "dp", scatter_dimension=0, tiled=True
            ).astype(jnp.float32),
            lax.psum_scatter(
                gain_two_part.astype(jnp.bfloat16), "dp", scatter_dimension=0, tiled=True
            ).astype(jnp.float32),
            lax.psum_scatter(
                shift_two_part.astype(jnp.bfloat16), "dp", scatter_dimension=0, tiled=True
            ).astype(jnp.float32),
            lax.psum_scatter(
                gain_three_part.astype(jnp.bfloat16), "dp", scatter_dimension=0, tiled=True
            ).astype(jnp.float32),
            lax.psum_scatter(
                shift_three_part.astype(jnp.bfloat16), "dp", scatter_dimension=0, tiled=True
            ).astype(jnp.float32),
        )
        kv_parts = (
            lax.psum_scatter(ckey_part, ("dp", "mem"), scatter_dimension=0, tiled=True),
            lax.psum_scatter(cvalue_part, ("dp", "mem"), scatter_dimension=0, tiled=True),
        )
        if summed is None:
            summed = tuple(shard_parts)
            kv_summed = tuple(kv_parts)
        else:
            summed = jax.tree.map(jnp.add, summed, tuple(shard_parts))
            kv_summed = jax.tree.map(jnp.add, kv_summed, tuple(kv_parts))
    return (
        jnp.concatenate(outputs, axis=0),
        jnp.concatenate(input_grads, axis=0),
        jnp.concatenate(memory_grads, axis=0),
        summed[0],
        summed[1],
        summed[2],
        summed[3],
        summed[4],
        kv_summed[0],
        kv_summed[1],
        summed[5],
        summed[6],
        summed[7],
        summed[8],
        summed[9],
        summed[10],
        summed[11],
        summed[12],
        summed[13],
    )


def solution(mesh):
    placed = (
        P("dp", None, None),
        P("dp", "mem", None),
        P("dp"),
        P("dp", None),
        P("dp", None),
        P("dp", None),
        P("dp", None),
        P("dp", None),
        P("dp", None),
        P("dp", None),
        P("dp", None),
        P("dp", None),
        P("dp", None),
        P(),
        P(),
        P(),
        P(),
        P(),
        P(),
        P("dp", None, None),
    )
    return jax.shard_map(
        on_device,
        mesh=mesh,
        in_specs=placed,
        out_specs=(
            P("dp", None, None),
            P("dp", None, None),
            P("dp", "mem", None),
            P("dp", None),
            P("dp", None),
            P("dp", None),
            P("dp", None),
            P("dp", None),
            P(("dp", "mem"), None),
            P(("dp", "mem"), None),
            P("dp", None),
            P("dp", None),
            P("dp", None),
            P("dp"),
            P("dp"),
            P("dp"),
            P("dp"),
            P("dp"),
            P("dp"),
        ),
        check_vma=False,
    )
```

profile of v0, /device:TPU:0, one launch (start us, length us, event | category | flops | bytes accessed | tf_op | source)
XLA Modules:
  0.0 2200.1 jit_solution(3231049925948016227)
XLA Ops:
  801.1 38.9 %reduce-scatter.123.cloned.1.call-done = bf16[96,768]{1,0:T(8,128)(2,1)} async-done(((bf16[768,768]{1,0:T(8,128)(2,1)}), bf16[96,768]{1,0:T(8,128)(2,1)}) %reduce-scatter.123.cloned.1.call-update) | async-done | bytes 147472
  841.2 39.2 %reduce-scatter.125.cloned.1.call-done = bf16[96,768]{1,0:T(8,128)(2,1)} async-done(((bf16[768,768]{1,0:T(8,128)(2,1)}), bf16[96,768]{1,0:T(8,128)(2,1)}) %reduce-scatter.125.cloned.1.call-update) | async-done | bytes 147472
  921.4 39.3 %reduce-scatter.113.cloned.1.call-done = bf16[96,768]{1,0:T(8,128)(2,1)} async-done(((bf16[768,768]{1,0:T(8,128)(2,1)}), bf16[96,768]{1,0:T(8,128)(2,1)}) %reduce-scatter.113.cloned.1.call-update) | async-done | bytes 147472
  961.8 38.9 %reduce-scatter.115.cloned.1.call-done = bf16[96,768]{1,0:T(8,128)(2,1)} async-done(((bf16[768,768]{1,0:T(8,128)(2,1)}), bf16[96,768]{1,0:T(8,128)(2,1)}) %reduce-scatter.115.cloned.1.call-update) | async-done | bytes 147472
  1001.8 39.2 %reduce-scatter.117.cloned.1.call-done = bf16[96,768]{1,0:T(8,128)(2,1)} async-done(((bf16[768,768]{1,0:T(8,128)(2,1)}), bf16[96,768]{1,0:T(8,128)(2,1)}) %reduce-scatter.117.cloned.1.call-update) | async-done | bytes 147472
  1082.1 39.2 %reduce-scatter.105.cloned.1.call-done = bf16[96,768]{1,0:T(8,128)(2,1)} async-done(((bf16[768,768]{1,0:T(8,128)(2,1)}), bf16[96,768]{1,0:T(8,128)(2,1)}) %reduce-scatter.105.cloned.1.call-update) | async-done | bytes 147472
  1122.3 39.4 %reduce-scatter.107.cloned.1.call-done = bf16[96,768]{1,0:T(8,128)(2,1)} async-done(((bf16[768,768]{1,0:T(8,128)(2,1)}), bf16[96,768]{1,0:T(8,128)(2,1)}) %reduce-scatter.107.cloned.1.call-update) | async-done | bytes 147472
  1162.8 39.9 %reduce-scatter.109.cloned.1.call-done = bf16[96,768]{1,0:T(8,128)(2,1)} async-done(((bf16[768,768]{1,0:T(8,128)(2,1)}), bf16[96,768]{1,0:T(8,128)(2,1)}) %reduce-scatter.109.cloned.1.call-update) | async-done | bytes 147472
  1242.6 40.2 %reduce-scatter.75.cloned.1.call-done = bf16[96,768]{1,0:T(8,128)(2,1)} async-done(((bf16[768,768]{1,0:T(8,128)(2,1)}), bf16[96,768]{1,0:T(8,128)(2,1)}) %reduce-scatter.75.cloned.1.call-update) | async-done | bytes 147472 | tf_op jit(solution)/shard_map/reduce_scatter | solution.py:272
  1282.9 40.0 %reduce-scatter.71.cloned.1.call-done = bf16[96,768]{1,0:T(8,128)(2,1)} async-done(((bf16[768,768]{1,0:T(8,128)(2,1)}), bf16[96,768]{1,0:T(8,128)(2,1)}) %reduce-scatter.71.cloned.1.call-update) | async-done | bytes 147472 | tf_op jit(solution)/shard_map/reduce_scatter | solution.py:272
  1322.8 40.4 %reduce-scatter.77.cloned.1.call-done = bf16[96,768]{1,0:T(8,128)(2,1)} async-done(((bf16[768,768]{1,0:T(8,128)(2,1)}), bf16[96,768]{1,0:T(8,128)(2,1)}) %reduce-scatter.77.cloned.1.call-update) | async-done | bytes 147472 | tf_op jit(solution)/shard_map/reduce_scatter | solution.py:272
  1403.1 40.4 %reduce-scatter.65.cloned.1.call-done = bf16[96,768]{1,0:T(8,128)(2,1)} async-done(((bf16[768,768]{1,0:T(8,128)(2,1)}), bf16[96,768]{1,0:T(8,128)(2,1)}) %reduce-scatter.65.cloned.1.call-update) | async-done | bytes 147472 | tf_op jit(solution)/shard_map/reduce_scatter | solution.py:269
  1443.4 40.0 %reduce-scatter.63.cloned.1.call-done = bf16[96,768]{1,0:T(8,128)(2,1)} async-done(((bf16[768,768]{1,0:T(8,128)(2,1)}), bf16[96,768]{1,0:T(8,128)(2,1)}) %reduce-scatter.63.cloned.1.call-update) | async-done | bytes 147472 | tf_op jit(solution)/shard_map/reduce_scatter | solution.py:269
  1483.4 40.2 %reduce-scatter.69.cloned.1.call-done = bf16[96,768]{1,0:T(8,128)(2,1)} async-done(((bf16[768,768]{1,0:T(8,128)(2,1)}), bf16[96,768]{1,0:T(8,128)(2,1)}) %reduce-scatter.69.cloned.1.call-update) | async-done | bytes 147472 | tf_op jit(solution)/shard_map/reduce_scatter | solution.py:269
  1525.5 55.3 %reduce-scatter.95.cloned.1.call-done = bf16[384,768]{1,0:T(8,128)(2,1)} async-done(((bf16[3072,768]{1,0:T(8,128)(2,1)}), bf16[384,768]{1,0:T(8,128)(2,1)}) %reduce-scatter.95.cloned.1.call-update) | async-done | bytes 589840 | tf_op jit(solution)/shard_map/reduce_scatter | solution.py:281
  1580.9 57.7 %reduce-scatter.97.cloned.1.call-done = bf16[384,768]{1,0:T(8,128)(2,1)} async-done(((bf16[3072,768]{1,0:T(8,128)(2,1)}), bf16[384,768]{1,0:T(8,128)(2,1)}) %reduce-scatter.97.cloned.1.call-update) | async-done | bytes 589840 | tf_op jit(solution)/shard_map/reduce_scatter | solution.py:281
  1638.6 57.2 %reduce-scatter.99.cloned.1.call-done = bf16[384,768]{1,0:T(8,128)(2,1)} async-done(((bf16[3072,768]{1,0:T(8,128)(2,1)}), bf16[384,768]{1,0:T(8,128)(2,1)}) %reduce-scatter.99.cloned.1.call-update) | async-done | bytes 589840 | tf_op jit(solution)/shard_map/reduce_scatter | solution.py:281
  1695.8 57.7 %reduce-scatter.101.cloned.1.call-done = bf16[384,768]{1,0:T(8,128)(2,1)} async-done(((bf16[3072,768]{1,0:T(8,128)(2,1)}), bf16[384,768]{1,0:T(8,128)(2,1)}) %reduce-scatter.101.cloned.1.call-update) | async-done | bytes 589840 | tf_op jit(solution)/shard_map/reduce_scatter | solution.py:281
  1756.5 54.5 %reduce-scatter.91.cloned.1.call-done = bf16[96,3072]{1,0:T(8,128)(2,1)} async-done(((bf16[768,3072]{1,0:T(8,128)(2,1)}), bf16[96,3072]{1,0:T(8,128)(2,1)}) %reduce-scatter.91.cloned.1.call-update) | async-done | bytes 589840 | tf_op jit(solution)/shard_map/reduce_scatter | solution.py:278
  1810.9 57.7 %reduce-scatter.89.cloned.1.call-done = bf16[96,3072]{1,0:T(8,128)(2,1)} async-done(((bf16[768,3072]{1,0:T(8,128)(2,1)}), bf16[96,3072]{1,0:T(8,128)(2,1)}) %reduce-scatter.89.cloned.1.call-update) | async-done | bytes 589840 | tf_op jit(solution)/shard_map/reduce_scatter | solution.py:278
  1868.7 57.2 %reduce-scatter.87.cloned.1.call-done = bf16[96,3072]{1,0:T(8,128)(2,1)} async-done(((bf16[768,3072]{1,0:T(8,128)(2,1)}), bf16[96,3072]{1,0:T(8,128)(2,1)}) %reduce-scatter.87.cloned.1.call-update) | async-done | bytes 589840 | tf_op jit(solution)/shard_map/reduce_scatter | solution.py:278
  1925.9 57.7 %reduce-scatter.93.cloned.1.call-done = bf16[96,3072]{1,0:T(8,128)(2,1)} async-done(((bf16[768,3072]{1,0:T(8,128)(2,1)}), bf16[96,3072]{1,0:T(8,128)(2,1)}) %reduce-scatter.93.cloned.1.call-update) | async-done | bytes 589840 | tf_op jit(solution)/shard_map/reduce_scatter | solution.py:278
  1986.6 101.8 %reduce-scatter.129.cloned.1.call-done = f32[24,768]{1,0:T(8,128)} async-done(((f32[768,768]{1,0:T(8,128)}), f32[24,768]{1,0:T(8,128)}) %reduce-scatter.129.cloned.1.call-update) | async-done | bytes 73744
  2088.4 104.7 %reduce-scatter.127.cloned.1.call-done = f32[24,768]{1,0:T(8,128)} async-done(((f32[768,768]{1,0:T(8,128)}), f32[24,768]{1,0:T(8,128)}) %reduce-scatter.127.cloned.1.call-update) | async-done | bytes 73744
  (1323 shorter events, 962.6 us)
Async XLA Ops:
  604.2 396.5 %reduce-scatter.115.cloned.1.call-start = ((), (), s32[]{:S(2)}) async-start(), calls=%async_computation.70 | async-start | bytes 1327104
  609.7 431.3 %reduce-scatter.117.cloned.1.call-start = ((), (), s32[]{:S(2)}) async-start(), calls=%async_computation.71 | async-start | bytes 1327104
  615.1 465.9 %reduce-scatter.103.cloned.1.call-start = ((), (), s32[]{:S(2)}) async-start(), calls=%async_computation.64 | async-start | bytes 1327104
  618.9 502.4 %reduce-scatter.105.cloned.1.call-start = ((), (), s32[]{:S(2)}) async-start(), calls=%async_computation.65 | async-start | bytes 1327104
  622.0 539.7 %reduce-scatter.107.cloned.1.call-start = ((), (), s32[]{:S(2)}) async-start(), calls=%async_computation.66 | async-start | bytes 1327104
  625.1 577.6 %reduce-scatter.109.cloned.1.call-start = ((), (), s32[]{:S(2)}) async-start(), calls=%async_computation.67 | async-start | bytes 1327104
  628.2 614.5 %reduce-scatter.73.cloned.1.call-start = ((), (), s32[]{:S(2)}) async-start(), calls=%async_computation.49 | async-start | bytes 1327104 | tf_op jit(solution)/shard_map/reduce_scatter | solution.py:272
  630.0 652.9 %reduce-scatter.75.cloned.1.call-start = ((), (), s32[]{:S(2)}) async-start(), calls=%async_computation.50 | async-start | bytes 1327104 | tf_op jit(solution)/shard_map/reduce_scatter | solution.py:272
  631.7 691.1 %reduce-scatter.71.cloned.1.call-start = ((), (), s32[]{:S(2)}) async-start(), calls=%async_computation.48 | async-start | bytes 1327104 | tf_op jit(solution)/shard_map/reduce_scatter | solution.py:272
  633.5 729.7 %reduce-scatter.77.cloned.1.call-start = ((), (), s32[]{:S(2)}) async-start(), calls=%async_computation.51 | async-start | bytes 1327104 | tf_op jit(solution)/shard_map/reduce_scatter | solution.py:272
  635.3 767.7 %reduce-scatter.67.cloned.1.call-start = ((), (), s32[]{:S(2)}) async-start(), calls=%async_computation.46 | async-start | bytes 1327104 | tf_op jit(solution)/shard_map/reduce_scatter | solution.py:269
  636.9 806.5 %reduce-scatter.65.cloned.1.call-start = ((), (), s32[]{:S(2)}) async-start(), calls=%async_computation.45 | async-start | bytes 1327104 | tf_op jit(solution)/shard_map/reduce_scatter | solution.py:269
  638.5 844.9 %reduce-scatter.63.cloned.1.call-start = ((), (), s32[]{:S(2)}) async-start(), calls=%async_computation.44 | async-start | bytes 1327104 | tf_op jit(solution)/shard_map/reduce_scatter | solution.py:269
  640.2 883.5 %reduce-scatter.69.cloned.1.call-start = ((), (), s32[]{:S(2)}) async-start(), calls=%async_computation.47 | async-start | bytes 1327104 | tf_op jit(solution)/shard_map/reduce_scatter | solution.py:269
  641.7 939.1 %reduce-scatter.95.cloned.1.call-start = ((), (), s32[]{:S(2)}) async-start(), calls=%async_computation.60 | async-start | bytes 5308416 | tf_op jit(solution)/shard_map/reduce_scatter | solution.py:281
  645.7 992.9 %reduce-scatter.97.cloned.1.call-start = ((), (), s32[]{:S(2)}) async-start(), calls=%async_computation.61 | async-start | bytes 5308416 | tf_op jit(solution)/shard_map/reduce_scatter | solution.py:281
  650.9 1044.9 %reduce-scatter.99.cloned.1.call-start = ((), (), s32[]{:S(2)}) async-start(), calls=%async_computation.62 | async-start | bytes 5308416 | tf_op jit(solution)/shard_map/reduce_scatter | solution.py:281
  656.1 1097.4 %reduce-scatter.101.cloned.1.call-start = ((), (), s32[]{:S(2)}) async-start(), calls=%async_computation.63 | async-start | bytes 5308416 | tf_op jit(solution)/shard_map/reduce_scatter | solution.py:281
  661.3 1149.6 %reduce-scatter.91.cloned.1.call-start = ((), (), s32[]{:S(2)}) async-start(), calls=%async_computation.58 | async-start | bytes 5308416 | tf_op jit(solution)/shard_map/reduce_scatter | solution.py:278
  666.2 1202.5 %reduce-scatter.89.cloned.1.call-start = ((), (), s32[]{:S(2)}) async-start(), calls=%async_computation.57 | async-start | bytes 5308416 | tf_op jit(solution)/shard_map/reduce_scatter | solution.py:278
  671.2 1254.7 %reduce-scatter.87.cloned.1.call-start = ((), (), s32[]{:S(2)}) async-start(), calls=%async_computation.56 | async-start | bytes 5308416 | tf_op jit(solution)/shard_map/reduce_scatter | solution.py:278
  676.0 1307.7 %reduce-scatter.93.cloned.1.call-start = ((), (), s32[]{:S(2)}) async-start(), calls=%async_computation.59 | async-start | bytes 5308416 | tf_op jit(solution)/shard_map/reduce_scatter | solution.py:278
  680.9 1407.5 %reduce-scatter.129.cloned.1.call-start = ((), (), s32[]{:S(2)}) async-start(), calls=%async_computation.77 | async-start | bytes 2433024
  694.8 1498.3 %reduce-scatter.127.cloned.1.call-start = ((), (), s32[]{:S(2)}) async-start(), calls=%async_computation.76 | async-start | bytes 2433024
  (459 other events, 6499.4 us)
Sparse Core Ops, SparseCore 0:
  299.1 43.2 all-reduce.34
  344.1 37.9 all-gather.26
  384.0 38.9 all-gather.28
  518.2 41.9 all-reduce.32
  602.7 36.7 reduce-scatter.84
  682.8 36.7 reduce-scatter.80
  722.7 37.0 reduce-scatter.118
  763.2 36.7 reduce-scatter.120
  843.5 36.7 reduce-scatter.124
  923.9 36.7 reduce-scatter.112
  1004.2 36.7 reduce-scatter.116
  1084.4 36.7 reduce-scatter.104
  1165.8 36.7 reduce-scatter.108
  1326.4 36.7 reduce-scatter.76
  1526.9 53.8 reduce-scatter.94
  1584.7 53.8 reduce-scatter.96
  1641.9 53.8 reduce-scatter.98
  1699.7 53.8 reduce-scatter.100
  1757.0 53.8 reduce-scatter.90
  1814.8 53.8 reduce-scatter.88
  1872.0 53.8 reduce-scatter.86
  1929.7 53.8 reduce-scatter.92
  1989.4 98.9 reduce-scatter.128
  2094.9 98.1 reduce-scatter.126
  (22 shorter events, 707.4 us)
where the time goes:
time: 2210 us; the launch traced here: 2200 us
  waiting for transfers between devices  1670 us (76%)
  matrix products  246 us (11%)
  local copies, waits for them, and re-layouts  132 us (6%)
  blocking collectives  80.3 us (4%)
  other arithmetic  53 us (2%)
    unnamed x60, waiting for transfers between devices  639 us
    reduce_scatter x4, waiting for transfers between devices, on_device(): lax.psum_scatter(contract_part.astype(jnp.bfloat16), 'dp', scatter_dimens...  228 us
    reduce_scatter x4, waiting for transfers between devices, on_device(): lax.psum_scatter(expand_part.astype(jnp.bfloat16), 'dp', scatter_dimensio...  227 us
    reduce_scatter x4, waiting for transfers between devices, on_device(): lax.psum_scatter(cquery_part.astype(jnp.bfloat16), 'dp', scatter_dimensio...  159 us
    reduce_scatter x4, waiting for transfers between devices, on_device(): lax.psum_scatter(out_part.astype(jnp.bfloat16), 'dp', scatter_dimension=0...  158 us
    unnamed x910, local copies, waits for them, and re-layouts  88.9 us
    dot_general x40, matrix products, project(): jnp.einsum('btd,df->btf', values, weight, preferred_element_type=jnp.floa...  69.6 us
    dot_general x40, matrix products, weight_grad(): jnp.einsum('btd,btf->df', left, right, preferred_element_type=jnp.float32)  63.1 us
  transfers between devices with their start and end apart: 46, of which 39 were waited for; matrix products, arithmetic and copies ran while one was open for 14% of the time, Pallas kernels for 0%

commit v1 on v0

v1 whole, which is shorter than its diff:
```python
import jax
import jax.numpy as jnp
from jax import lax
from jax.sharding import PartitionSpec as P

H = 12
LOW = jnp.bfloat16
WIDE = jnp.float32


def mm(a, b, dims):
    return lax.dot_general(a, b, (dims, ((), ())), preferred_element_type=WIDE)


def project(values, weight):
    return mm(values, weight, ((1,), (0,)))


def back_project(grads, weight):
    return mm(grads, weight, ((1,), (1,)))


def weight_grad(left, right):
    return mm(left, right, ((0,), (0,)))


def heads_of(values, images):
    rows, width = values.shape
    return values.reshape(images, rows // images, H, width // H)


def norm_forward(resid, gain, shift):
    center = resid - jnp.mean(resid, axis=-1, keepdims=True)
    inverse = lax.rsqrt(jnp.mean(center * center, axis=-1, keepdims=True) + 1e-05)
    normed = center * inverse
    return (normed * gain + shift, normed, inverse)


def norm_backward(incoming, normed, inverse, gain):
    scaled = incoming * gain
    grad_in = inverse * (
        scaled
        - jnp.mean(scaled, axis=-1, keepdims=True)
        - normed * jnp.mean(scaled * normed, axis=-1, keepdims=True)
    )
    return (grad_in, jnp.sum(incoming * normed, axis=0), jnp.sum(incoming, axis=0))


def scores_of(query, keys):
    return jnp.einsum("bqhe,bkhe->bhqk", query, keys, preferred_element_type=WIDE) * 0.125


def mix(probs, values):
    return jnp.einsum("bhqk,bkhe->bqhe", probs, values, preferred_element_type=WIDE)


def mix_back(probs, grads):
    return jnp.einsum("bhqk,bqhe->bkhe", probs, grads, preferred_element_type=WIDE)


def attention_backward(probs, attn, grad_attn, query, keys, values):
    row = jnp.sum(grad_attn.astype(WIDE) * attn.astype(WIDE), axis=-1).transpose(0, 2, 1)[..., None]
    grad_probs = jnp.einsum("bqhe,bkhe->bhqk", grad_attn, values, preferred_element_type=WIDE)
    grad_scores = (probs * (grad_probs - row)).astype(LOW)
    grad_query = mix(grad_scores, keys) * 0.125
    grad_keys = mix_back(grad_scores, query) * 0.125
    grad_values = mix_back(probs.astype(LOW), grad_attn)
    return (grad_query, grad_keys, grad_values)


def gelu_tanh(values):
    return jax.nn.gelu(values, approximate=True)


def on_device(
    inputs,
    memory,
    lengths,
    self_query,
    self_key,
    self_value,
    self_out,
    cross_query,
    cross_key,
    cross_value,
    cross_out,
    expand_weight,
    contract_weight,
    gain_one,
    shift_one,
    gain_two,
    shift_two,
    gain_three,
    shift_three,
    cotangent,
):
    images, queries, width = inputs.shape
    mem_rows = memory.shape[1]
    rows = images * queries
    share = self_query.shape[0]
    parts = width // share
    squares = (self_query, self_key, self_value, self_out, cross_query, cross_key, cross_value, cross_out)
    packed = lax.all_gather(jnp.stack(squares), "dp", axis=1, tiled=True)
    expand_full = lax.all_gather(expand_weight, "dp", axis=0, tiled=True)
    contract_full = lax.all_gather(contract_weight, "dp", axis=0, tiled=True)
    (query_full, key_full, value_full, out_full, cquery_full, ckey_full, cvalue_full, cout_full) = packed
    tokens = inputs.reshape(rows, width)
    memory_flat = memory.reshape(images * mem_rows, width)
    incoming = cotangent.reshape(rows, width).astype(WIDE)

    def joined(values):
        return values.reshape(-1, width)

    query_heads = heads_of(project(tokens, query_full).astype(LOW), images)
    key_heads = heads_of(project(tokens, key_full).astype(LOW), images)
    value_heads = heads_of(project(tokens, value_full).astype(LOW), images)
    self_raw = scores_of(query_heads, key_heads)
    self_exp = jnp.exp(self_raw - jnp.max(self_raw, axis=-1, keepdims=True))
    self_probs = self_exp / jnp.sum(self_exp, axis=-1, keepdims=True)
    self_attn = joined(mix(self_probs.astype(LOW), value_heads)).astype(LOW)
    first, normed_one, inverse_one = norm_forward(
        tokens.astype(WIDE) + project(self_attn, out_full), gain_one, shift_one
    )
    first_low = first.astype(LOW)
    cross_q = heads_of(project(first_low, cquery_full).astype(LOW), images)
    cross_k = heads_of(project(memory_flat, ckey_full).astype(LOW), images)
    cross_v = heads_of(project(memory_flat, cvalue_full).astype(LOW), images)
    places = lax.axis_index("mem") * mem_rows + jnp.arange(mem_rows, dtype=jnp.int32)
    valid = (places[None, :] < lengths[:, None])[:, None, None, :]
    cross_raw = jnp.where(valid, scores_of(cross_q, cross_k), -1e30)
    top = lax.pmax(jnp.max(cross_raw, axis=-1, keepdims=True), "mem")
    cross_exp = jnp.where(valid, jnp.exp(cross_raw - top), 0.0)
    total = lax.psum(jnp.sum(cross_exp, axis=-1, keepdims=True), "mem")
    cross_probs = cross_exp / total
    cross_attn = lax.psum(joined(mix(cross_probs.astype(LOW), cross_v)).astype(LOW), "mem")
    second, normed_two, inverse_two = norm_forward(
        first + project(cross_attn, cout_full), gain_two, shift_two
    )
    second_low = second.astype(LOW)
    pre_act = project(second_low, expand_full)
    activ, gelu_pull = jax.vjp(gelu_tanh, pre_act)
    activ_low = activ.astype(LOW)
    result, normed_three, inverse_three = norm_forward(
        second + project(activ_low, contract_full), gain_three, shift_three
    )
    grad_three, gain_three_part, shift_three_part = norm_backward(
        incoming, normed_three, inverse_three, gain_three
    )
    grad_ffn = grad_three.astype(LOW)

    def scattered(part, axes="dp"):
        return lax.psum_scatter(part, axes, scatter_dimension=0, tiled=True).astype(WIDE)

    contract_grad = scattered(weight_grad(activ_low, grad_ffn).astype(LOW))
    grad_pre = gelu_pull(back_project(grad_ffn, contract_full))[0].astype(LOW)
    expand_grad = scattered(weight_grad(second_low, grad_pre).astype(LOW))
    grad_second = grad_three + back_project(grad_pre, expand_full)
    grad_two, gain_two_part, shift_two_part = norm_backward(
        grad_second, normed_two, inverse_two, gain_two
    )
    grad_cross = grad_two.astype(LOW)
    cout_part = weight_grad(cross_attn, grad_cross)
    grad_cattn = heads_of(back_project(grad_cross, cout_full).astype(LOW), images)
    part_cquery, grad_ckey, grad_cvalue = attention_backward(
        cross_probs, heads_of(cross_attn, images), grad_cattn, cross_q, cross_k, cross_v
    )
    grad_cquery = lax.psum(joined(part_cquery).astype(LOW), "mem")
    grad_ckey = joined(grad_ckey).astype(LOW)
    grad_cvalue = joined(grad_cvalue).astype(LOW)
    kv_grad = scattered(
        jnp.concatenate(
            [weight_grad(memory_flat, grad_ckey), weight_grad(memory_flat, grad_cvalue)], axis=1
        ).astype(LOW),
        ("dp", "mem"),
    )
    memory_grad = back_project(grad_ckey, ckey_full) + back_project(grad_cvalue, cvalue_full)
    cquery_part = weight_grad(first_low, grad_cquery)
    grad_first = grad_two + back_project(grad_cquery, cquery_full)
    grad_one, gain_one_part, shift_one_part = norm_backward(
        grad_first, normed_one, inverse_one, gain_one
    )
    grad_self = grad_one.astype(LOW)
    out_part = weight_grad(self_attn, grad_self)
    grad_sattn = heads_of(back_project(grad_self, out_full).astype(LOW), images)
    grad_query, grad_key, grad_value = (
        joined(grad).astype(LOW)
        for grad in attention_backward(
            self_probs, heads_of(self_attn, images), grad_sattn, query_heads, key_heads, value_heads
        )
    )
    input_grad = (
        grad_one
        + back_project(grad_query, query_full)
        + back_project(grad_key, key_full)
        + back_project(grad_value, value_full)
    )
    norm_parts = jnp.stack(
        [gain_one_part, shift_one_part, gain_two_part, shift_two_part, gain_three_part, shift_three_part], axis=1
    )
    rest = scattered(
        jnp.concatenate(
            [
                weight_grad(tokens, grad_query),
                weight_grad(tokens, grad_key),
                weight_grad(tokens, grad_value),
                out_part,
                cquery_part,
                cout_part,
                jnp.pad(norm_parts, ((0, 0), (0, 122))),
            ],
            axis=1,
        ).astype(LOW)
    )
    squares_grad = [rest[:, place * width : (place + 1) * width] for place in range(6)]
    norms_grad = [rest[:, 6 * width + place] for place in range(6)]
    return (
        result.reshape(inputs.shape),
        input_grad.reshape(inputs.shape),
        memory_grad.reshape(memory.shape),
        *squares_grad[:5],
        kv_grad[:, :width],
        kv_grad[:, width:],
        squares_grad[5],
        expand_grad,
        contract_grad,
        *norms_grad,
    )


def solution(mesh):
    rows = P("dp", None)
    image = P("dp", None, None)
    token = P("dp", "mem", None)
    both = P(("dp", "mem"), None)
    return jax.shard_map(
        on_device,
        mesh=mesh,
        in_specs=(image, token, P("dp"), *[rows] * 10, *[P()] * 6, image),
        out_specs=(image, image, token, *[rows] * 5, both, both, *[rows] * 3, *[P("dp")] * 6),
        check_vma=False,
    )
```

time: 2210 us -> 723 us (0.33)
  waiting for transfers between devices: 1670 us -> 361 us
  matrix products: 246 us -> 145 us
  blocking collectives: 80.3 us -> 34.8 us
  other arithmetic: 53 us -> 20.4 us
    reduce_scatter x20 -> x2, waiting for transfers between devices: 772 us -> 109 us  [scattered(): lax.psum_scatter(part, axes, scatter_dimension=0, tiled=True).astype(WIDE)]
    unnamed x60 -> x11, waiting for transfers between devices: 639 us -> 85.9 us
    dot_general x164 -> x41, matrix products: 238 us -> 141 us  [the longest x30 102 us: mm(): return lax.dot_general(a, b, (dims, ((), ())), preferred_element_type=WIDE)]
    all_gather x10 -> x3, waiting for transfers between devices: 180 us -> 130 us  [the longest x1 60.3 us: on_device(): packed = lax.all_gather(jnp.stack(squares), 'dp', axis=1, tiled=True)]
    reshape x0 -> x16, local copies, waits for them, and re-layouts: none -> 42.3 us  [the longest x13 38.3 us: heads_of(): return values.reshape(images, rows // images, H, width // H)]
    unnamed x910 -> x127, local copies, waits for them, and re-layouts: 88.9 us -> 47.8 us
    psum x2, waiting for transfers between devices: 73.9 us -> 36.2 us  [the longest x1 36.2 us: on_device(): lax.psum(joined(mix(cross_probs.astype(LOW), cross_v)).astype(LOW), 'mem')]
    unnamed x1 -> x0, blocking collectives: 25.3 us -> none
  transfers between devices with their start and end apart: 46 -> 9, of which waited for: 39 -> 8; matrix products, arithmetic and copies ran while one was open for 14% -> 21% of each run, Pallas kernels for 0% -> 0%
where the time goes in v1:
time: 723 us; the launch traced here: 718 us
  waiting for transfers between devices  361 us (50%)
  matrix products  145 us (20%)
  local copies, waits for them, and re-layouts  141 us (20%)
  blocking collectives  34.8 us (5%)
  other arithmetic  20.4 us (3%)
  between operations  15 us (2%)
    reduce_scatter x2, waiting for transfers between devices, scattered(): lax.psum_scatter(part, axes, scatter_dimension=0, tiled=True).astype(WIDE)  109 us
    dot_general x30, matrix products, mm(): return lax.dot_general(a, b, (dims, ((), ())), preferred_element_type=WIDE)  102 us
    unnamed x11, waiting for transfers between devices  85.9 us
    all_gather x1, waiting for transfers between devices, on_device(): packed = lax.all_gather(jnp.stack(squares), 'dp', axis=1, tiled=True)  60.3 us
    unnamed x127, local copies, waits for them, and re-layouts  47.8 us
    reshape x13, local copies, waits for them, and re-layouts, heads_of(): return values.reshape(images, rows // images, H, width // H)  38.3 us
    psum x1, waiting for transfers between devices, on_device(): lax.psum(joined(mix(cross_probs.astype(LOW), cross_v)).astype(LOW), 'mem')  36.2 us
    all_gather x1, waiting for transfers between devices, on_device(): expand_full = lax.all_gather(expand_weight, 'dp', axis=0, tiled=True)  36.1 us
  transfers between devices with their start and end apart: 9, of which 8 were waited for; matrix products, arithmetic and copies ran while one was open for 21% of the time, Pallas kernels for 0%

profile of v1, /device:TPU:0, one launch (start us, length us, event | category | flops | bytes accessed | tf_op | source)
XLA Modules:
  0.0 718.2 jit_solution(10065242548972240690)
XLA Ops:
  16.4 60.3 %all-gather.4.cloned.1.call-done = bf16[8,768,768]{2,1,0:T(8,128)(2,1)} async-done(((bf16[8,96,768]{2,1,0:T(8,128)(2,1)}), bf16[8,768,768]{2,1,0:T(8,128)(2,1)}) %all-gather.4.cloned.1.call-update) | async-done | bytes 9437200 | tf_op jit(solution)/shard_map/all_gather | solution.py:103
  81.0 5.3 reshape.218
  129.7 5.1 reshape.220
  134.8 6.5 fusion.1
  141.3 19.0 %pmax.7 = f32[4,12,100]{2,1,0:T(8,128)S(1)} all-reduce(f32[4,12,100]{2,1,0:T(8,128)S(1)} %get-tuple-element.144), channel_id=1, replica_groups=mesh['dp'=8,'mem'=4] {'mem'}, use_global_device_ids=true, to_apply=%region_5.6 | all-reduce | flops 4800 | bytes 38400 | tf_op jit(solution)/shard_map/pmax | solution.py:131
  164.7 15.9 %psum.21 = f32[4,12,100]{2,1,0:T(8,128)S(1)} all-reduce(f32[4,12,100]{2,1,0:T(8,128)S(1)} %fusion.3), channel_id=1, replica_groups=mesh['dp'=8,'mem'=4] {'mem'}, use_global_device_ids=true, to_apply=%region_7.8 | all-reduce | flops 4800 | bytes 38400 | tf_op jit(solution)/shard_map/psum | solution.py:133
  180.6 5.3 fusion.44
  196.0 36.2 %all-reduce.4.cloned.1.call-done = bf16[400,768]{0,1:T(8,128)(2,1)} async-done(((bf16[400,768]{0,1:T(8,128)(2,1)}), bf16[400,768]{0,1:T(8,128)(2,1)}) %all-reduce.4.cloned.1.call-update) | async-done | bytes 614416 | tf_op jit(solution)/shard_map/psum | solution.py:135
  236.2 36.1 %all-gather.6.cloned.1.call-done = bf16[768,3072]{1,0:T(8,128)(2,1)} async-done(((bf16[96,3072]{1,0:T(8,128)(2,1)}), bf16[768,3072]{1,0:T(8,128)(2,1)}) %all-gather.6.cloned.1.call-update) | async-done | bytes 4718608 | tf_op jit(solution)/shard_map/all_gather | solution.py:104
  272.3 7.2 fusion.79
  279.5 33.5 %all-gather.8.cloned.1.call-done = bf16[3072,768]{1,0:T(8,128)(2,1)} async-done(((bf16[384,768]{1,0:T(8,128)(2,1)}), bf16[3072,768]{1,0:T(8,128)(2,1)}) %all-gather.8.cloned.1.call-update) | async-done | bytes 4718608 | tf_op jit(solution)/shard_map/all_gather | solution.py:105
  313.0 7.3 %fusion.92 = (f32[400]{0:T(512)S(1)}, f32[400,768]{1,0:T(8,128)S(1)}) fusion(bf16[3072,768]{1,0:T(8,128)(2,1)} %all-gather.8.cloned.1.call-done, f32[400,3072]{1,0:T(8,128)} %fusion.79, f32[768]{0:T(1024)S(1)} %copy-done.43, f32[768]{0:T(1024)S(1)} %copy-done.38, f32[400]{0:T(512)S(1)} %add_rsqrt_fusion.1, f32[400,768]{1,0:T(8,128)} %copy-done.10, ...), kind=kOutput, calls=%fused_computation.172 | convolution fusion | flops 1900338816 | bytes 12102336 | tf_op jit(solution)/shard_map/dot_general | solution.py:12
  324.4 4.9 fusion.10
  346.7 6.6 multiply_convert_fusion
  364.6 4.9 copy.254
  374.2 4.9 copy.256
  395.0 7.0 convolution_convert_fusion.1
  402.3 8.0 %convolution_convert_fusion = bf16[3072,768]{1,0:T(8,128)(2,1)} fusion(f32[400,768]{1,0:T(8,128)} %copy-done.29, f32[400,3072]{1,0:T(8,128)} %fusion.79), kind=kOutput, calls=%fused_computation.9 | convolution fusion | flops 1901162496 | bytes 10862592 | tf_op jit(solution)/shard_map/dot_general | solution.py:12
  461.2 10.1 %copy.272 = bf16[768,4736]{1,0:T(8,128)(2,1)} copy(bf16[768,4736]{0,1:T(8,128)(2,1)} %pad_dynamic-update-slice_fusion) | data formatting | bytes 14548992
  480.0 5.2 convolution_add_fusion
  495.7 16.2 %reduce-scatter.15.cloned.1.call-done = bf16[24,1536]{1,0:T(8,128)(2,1)} async-done(((bf16[768,1536]{1,0:T(8,128)(2,1)}), bf16[24,1536]{1,0:T(8,128)(2,1)}) %reduce-scatter.15.cloned.1.call-update) | async-done | bytes 73744
  514.6 54.0 %reduce-scatter.9.cloned.1.call-done = bf16[96,3072]{1,0:T(8,128)(2,1)} async-done(((bf16[768,3072]{1,0:T(8,128)(2,1)}), bf16[96,3072]{1,0:T(8,128)(2,1)}) %reduce-scatter.9.cloned.1.call-update) | async-done | bytes 589840 | tf_op jit(solution)/shard_map/reduce_scatter | solution.py:152
  570.8 55.2 %reduce-scatter.11.cloned.1.call-done = bf16[384,768]{1,0:T(8,128)(2,1)} async-done(((bf16[3072,768]{1,0:T(8,128)(2,1)}), bf16[384,768]{1,0:T(8,128)(2,1)}) %reduce-scatter.11.cloned.1.call-update) | async-done | bytes 589840 | tf_op jit(solution)/shard_map/reduce_scatter | solution.py:152
  628.1 68.3 %reduce-scatter.13.cloned.1.call-done = bf16[96,4736]{1,0:T(8,128)(2,1)} async-done(((bf16[768,4736]{1,0:T(8,128)(2,1)}), bf16[96,4736]{1,0:T(8,128)(2,1)}) %reduce-scatter.13.cloned.1.call-update) | async-done | bytes 909328
  (255 shorter events, 220.2 us)
Async XLA Ops:
  7.2 69.5 %copy-start = (bf16[4,320,768]{2,1,0:T(8,128)(2,1)S(1)}, bf16[4,320,768]{2,1,0:T(8,128)(2,1)}, u32[]{:S(2)}) copy-start(bf16[4,320,768]{2,1,0:T(8,128)(2,1)} %param.21) | copy-start | bytes 5898244
  7.2 6.7 copy-start.35
  7.2 69.5 %all-gather.4.cloned.1.call-start = ((), (), s32[]{:S(2)}) async-start(), calls=%async_computation.4 | async-start | bytes 10616832 | tf_op jit(solution)/shard_map/all_gather | solution.py:103
  15.0 217.1 %all-reduce.4.cloned.1.call-start = ((), (), s32[]{:S(2)}) async-start(), calls=%async_computation.5 | async-start | bytes 1572864 | tf_op jit(solution)/shard_map/psum | solution.py:135
  16.3 82.9 %copy-start.33 = (bf16[400,768]{1,0:T(8,128)(2,1)}, bf16[400,768]{1,0:T(8,128)(2,1)S(1)}, u32[]{:S(2)}) copy-start(bf16[400,768]{1,0:T(8,128)(2,1)S(1)} %reshape.213) | copy-start | bytes 1843204
  99.2 8.4 %copy-start.14 = (bf16[4,100,12,64]{1,3,2,0:T(8,128)(2,1)}, bf16[4,100,12,64]{1,3,2,0:T(8,128)(2,1)S(1)}, u32[]{:S(2)}) copy-start(bf16[4,100,12,64]{1,3,2,0:T(8,128)(2,1)S(1)} %copy.221) | copy-start | bytes 1843204
  189.9 82.4 %all-gather.6.cloned.1.call-start = ((), (), s32[]{:S(2)}) async-start(), calls=%async_computation.6 | async-start | bytes 5308416 | tf_op jit(solution)/shard_map/all_gather | solution.py:104
  190.6 122.4 %all-gather.8.cloned.1.call-start = ((), (), s32[]{:S(2)}) async-start(), calls=%async_computation.7 | async-start | bytes 5308416 | tf_op jit(solution)/shard_map/all_gather | solution.py:105
  191.2 219.6 %all-reduce.6.cloned.1.call-start = ((), (), s32[]{:S(2)}) async-start(), calls=%async_computation.8 | async-start | bytes 1572864 | tf_op jit(solution)/shard_map/psum | solution.py:167
  196.0 76.3 %copy-start.38 = (f32[768]{0:T(1024)S(1)}, f32[768]{0:T(1024)}, u32[]{:S(2)}) copy-start(f32[768]{0:T(1024)} %param.35) | copy-start | bytes 9220
  196.0 76.3 %copy-start.43 = (f32[768]{0:T(1024)S(1)}, f32[768]{0:T(1024)}, u32[]{:S(2)}) copy-start(f32[768]{0:T(1024)} %param.36) | copy-start | bytes 9220
  313.0 10.7 %copy-start.46 = (f32[400,3072]{1,0:T(8,128)S(1)}, f32[400,3072]{1,0:T(8,128)}, u32[]{:S(2)}) copy-start(f32[400,3072]{1,0:T(8,128)} %fusion.79) | copy-start | bytes 14745604
  322.2 7.2 slice-start.2
  323.7 5.6 copy-start.29
  324.4 5.0 slice-start.3
  346.7 6.7 copy-start.1
  364.5 147.4 %reduce-scatter.15.cloned.1.call-start = ((), (), s32[]{:S(2)}) async-start(), calls=%async_computation.12 | async-start | bytes 2433024
  395.0 173.6 %reduce-scatter.9.cloned.1.call-start = ((), (), s32[]{:S(2)}) async-start(), calls=%async_computation.9 | async-start | bytes 5308416 | tf_op jit(solution)/shard_map/reduce_scatter | solution.py:152
  402.1 223.9 %reduce-scatter.11.cloned.1.call-start = ((), (), s32[]{:S(2)}) async-start(), calls=%async_computation.10 | async-start | bytes 5308416 | tf_op jit(solution)/shard_map/reduce_scatter | solution.py:152
  410.4 286.1 %reduce-scatter.13.cloned.1.call-start = ((), (), s32[]{:S(2)}) async-start(), calls=%async_computation.11 | async-start | bytes 8183808
  480.0 5.2 copy-start.17
  701.7 5.7 copy-start.27
  701.7 6.6 copy-start.26
  701.7 7.5 %copy-start.25 = (f32[96,768]{0,1:T(8,128)S(1)}, f32[96,768]{0,1:T(8,128)}, u32[]{:S(2)}) copy-start(f32[96,768]{0,1:T(8,128)} %get-tuple-element.132) | copy-start | bytes 884740
  (37 other events, 97.3 us)
Sparse Core Ops, SparseCore 0:
  15.1 61.5 all-gather.3
  190.0 42.0 all-reduce.3
  234.0 38.2 all-gather.5
  274.0 38.9 all-gather.7
  364.6 43.6 all-reduce.5
  413.5 98.3 reduce-scatter.14
  515.7 52.8 reduce-scatter.8
  572.1 53.8 reduce-scatter.10
  629.8 66.6 reduce-scatter.12

commit v2 on v1

--- a/solution.py
+++ b/solution.py
@@ -1,6 +1,9 @@
+import functools
 import jax
 import jax.numpy as jnp
 from jax import lax
+from jax.experimental import pallas as pl
+from jax.experimental.pallas import tpu as pltpu
 from jax.sharding import PartitionSpec as P
 
 H = 12
@@ -8,20 +11,20 @@
 WIDE = jnp.float32
 
 
-def mm(a, b, dims):
+def contract(a, b, dims):
     return lax.dot_general(a, b, (dims, ((), ())), preferred_element_type=WIDE)
 
 
 def project(values, weight):
-    return mm(values, weight, ((1,), (0,)))
+    return contract(values, weight, ((1,), (0,)))
 
 
 def back_project(grads, weight):
-    return mm(grads, weight, ((1,), (1,)))
+    return contract(grads, weight, ((1,), (1,)))
 
 
 def weight_grad(left, right):
-    return mm(left, right, ((0,), (0,)))
+    return contract(left, right, ((0,), (0,)))
 
 
 def heads_of(values, images):
@@ -227,13 +230,591 @@
     )
 
 
+MESH = pl.DeviceIdType.MESH
+ANY = pl.BlockSpec(memory_space=pl.ANY)
+INNER = pl.BlockSpec(memory_space=pltpu.VMEM)
+SCALAR = pl.BlockSpec(memory_space=pltpu.SMEM)
+D = 768
+FF = 3072
+PAIRS = 6
+QP = 112
+PIECES = 16
+SQ, SK, SV, SO, CK, CV, CQ, CO, EX, CT = 0, 1, 2, 3, 4, 5, 6, 7, 8, 12
+WINDOW = 4
+VMEM_BYTES = 60 * 2**20
+
+
+def mm(a, b):
+    return lax.dot_general(a, b, (((1,), (0,)), ((), ())), preferred_element_type=WIDE)
+
+
+def mm_nt(a, b):
+    return lax.dot_general(a, b, (((1,), (1,)), ((), ())), preferred_element_type=WIDE)
+
+
+def mm_tn(a, b):
+    return lax.dot_general(a, b, (((0,), (0,)), ((), ())), preferred_element_type=WIDE)
+
+
+def low_lanes(shape):
+    return lax.broadcasted_iota(jnp.int32, shape, 1) < 64
+
+
+def two_heads(pair):
+    lower = low_lanes(pair.shape)
+    nought = jnp.zeros_like(pair)
+    return jnp.concatenate([jnp.where(lower, pair, nought), jnp.where(lower, nought, pair)], axis=0)
+
+
+def one_pair(both):
+    rows = both.shape[0] // 2
+    upper = both[rows:]
+    return jnp.where(low_lanes(upper.shape), both[:rows], upper)
+
+
+def places():
+    d = lax.axis_index("dp")
+    c = lax.rem(d, 2)
+    x = lax.rem(d // 2, 2)
+    y = d // 4
+    other = d + 1 - 2 * c
+    beside = d + 2 - 4 * x
+    above = d + 4 - 8 * y
+    across = beside + 4 - 8 * y
+    return d, other, beside, above, across
+
+
+def weight_row(piece, owner):
+    if piece < CT:
+        return pl.multiple_of(piece * D + owner * 96, 96)
+    return pl.multiple_of(CT * D + owner * 384 + (piece - CT) * 96, 96)
+
+
+class Gather:
+    def __init__(self, shards, full, local, send, recv):
+        self.shards, self.full = shards, full
+        self.local, self.send, self.recv = local, send, recv
+        self.d, self.other, self.beside, self.above, self.across = places()
+        self.z = lax.axis_index("mem")
+        self.sent = []
+        self.done = 0
+        self.landed = [False] * PIECES
+
+    def at(self, piece, owner):
+        return self.full.at[pl.ds(weight_row(piece, owner), 96)]
+
+    def own(self, piece):
+        if piece < EX:
+            return self.shards[piece]
+        if piece < CT:
+            return self.shards[EX].at[:, pl.ds((piece - EX) * D, D)]
+        return self.shards[EX + 1].at[pl.ds((piece - CT) * 96, 96)]
+
+    def copy(self, src, piece, owner, kind, target):
+        return pltpu.make_async_remote_copy(
+            src,
+            self.at(piece, owner),
+            self.send.at[piece, kind],
+            self.recv.at[piece, kind],
+            device_id=(target, self.z),
+            device_id_type=MESH,
+        )
+
+    def push(self, src, piece, owner, kind, target):
+        one = self.copy(src, piece, owner, kind, target)
+        one.start()
+        self.sent.append(one)
+
+    def arrived(self, piece, kind):
+        self.copy(self.at(piece, self.d), piece, self.d, kind, self.other).wait_recv()
+
+    def start(self, piece):
+        if piece >= PIECES:
+            return
+        src = self.own(piece)
+        pltpu.make_async_copy(src, self.at(piece, self.d), self.local.at[piece]).start()
+        self.push(src, piece, self.d, 0, self.beside)
+        self.push(src, piece, self.d, 1, self.above)
+        self.push(src, piece, self.d, 3, self.other)
+
+    def begin(self):
+        for piece in range(WINDOW):
+            self.start(piece)
+
+    def finish(self, piece):
+        self.arrived(piece, 2)
+        self.push(self.at(piece, self.across), piece, self.across, 6, self.other)
+
+    def step(self):
+        piece = self.done
+        if piece > PIECES:
+            return
+        self.done += 1
+        if piece < PIECES:
+            self.arrived(piece, 0)
+            if piece % 2 == 0:
+                self.push(self.at(piece, self.beside), piece, self.beside, 2, self.above)
+            self.push(self.at(piece, self.beside), piece, self.beside, 4, self.other)
+            self.arrived(piece, 1)
+            if piece % 2 == 1:
+                self.push(self.at(piece, self.above), piece, self.above, 2, self.beside)
+            self.push(self.at(piece, self.above), piece, self.above, 5, self.other)
+            self.start(piece + WINDOW)
+        if piece >= 1:
+            self.finish(piece - 1)
+
+    def ready(self, piece):
+        while self.done <= piece + 1:
+            self.step()
+        if self.landed[piece]:
+            return
+        self.landed[piece] = True
+        pltpu.make_async_copy(self.own(piece), self.at(piece, self.d), self.local.at[piece]).wait()
+        for kind in range(3, 7):
+            self.arrived(piece, kind)
+
+    def close(self):
+        for one in self.sent:
+            one.wait_send()
+
+
+def greet(targets):
+    barrier = pltpu.get_barrier_semaphore()
+    for target in targets:
+        pl.semaphore_signal(barrier, 1, device_id=target, device_id_type=MESH)
+    pl.semaphore_wait(barrier, len(targets))
+
+
+def norm_rows(resid, gain, shift):
+    center = resid - jnp.mean(resid, axis=-1, keepdims=True)
+    inverse = lax.rsqrt(jnp.mean(center * center, axis=-1, keepdims=True) + 1e-05)
+    normed = center * inverse
+    return normed * gain + shift, normed, inverse
+
+
+def forward_kernel(images, queries, mem_rows, *refs):
+    (tok, mem, lens, norms, *rest) = refs
+    shards = rest[:10]
+    (o_result, o_full, o_acts, o_ffn, o_us, o_inv, o_kv, o_pc, o_ps, o_wst) = rest[10:20]
+    (
+        full, acts, ffn, us, inv, kv, pc, ps, wst, wide, stats, osend, orecv, srecv, fst,
+        local, send, recv, zsend, zrecv, keep,
+    ) = rest[20:]
+    rows = images * QP
+    z = lax.axis_index("mem")
+    d = lax.axis_index("dp")
+    gather = Gather(shards, full, local, send, recv)
+    others = [lax.rem(z + r, 4) for r in range(1, 4)]
+    greet(
+        [(gather.other, z), (gather.beside, z), (gather.above, z)] + [(d, other) for other in others]
+    )
+    gather.begin()
+    kept = []
+
+    def save(src, dst):
+        one = pltpu.make_async_copy(src, dst, keep.at[len(kept)])
+        one.start()
+        kept.append(one)
+
+    def weight(piece, tile):
+        return full[pl.ds(piece * D, D), pl.ds(pl.multiple_of(tile * 256, 256), 256)]
+
+    def cols(tile):
+        return pl.ds(pl.multiple_of(tile * 256, 256), 256)
+
+    def image(i):
+        return pl.ds(pl.multiple_of(i * QP, QP), QP)
+
+    def project_rows(src, piece, dst, scale):
+        def body(tile, carry):
+            out = mm(src[...], weight(piece, tile)).astype(LOW)
+            if scale != 1.0:
+                out = out * jnp.asarray(scale, LOW)
+            acts[dst, :, cols(tile)] = out
+            return carry
+
+        lax.fori_loop(0, 3, body, 0)
+
+    gather.ready(SQ)
+    project_rows(tok, SQ, 0, 0.125)
+    gather.ready(SK)
+    project_rows(tok, SK, 1, 1.0)
+    gather.ready(SV)
+    project_rows(tok, SV, 2, 1.0)
+
+    def self_image(i, carry):
+        at = image(i)
+        valid = lax.broadcasted_iota(jnp.int32, (2 * QP, QP), 1) < queries
+        for hp in range(PAIRS):
+            lanes = pl.ds(hp * 128, 128)
+            scores = mm_nt(two_heads(acts[0, at, lanes]), acts[1, at, lanes])
+            scores = jnp.where(valid, scores, -1e30)
+            grown = jnp.exp(scores - jnp.max(scores, axis=-1, keepdims=True))
+            probs = (grown / jnp.sum(grown, axis=-1, keepdims=True)).astype(LOW)
+            ps[i, hp] = probs
+            acts[3, at, lanes] = one_pair(mm(probs, acts[2, at, lanes])).astype(LOW)
+        return carry
+
+    lax.fori_loop(0, images, self_image, 0)
+    gather.step()
+
+    def memory_rows(piece, dst):
+        def body(i, carry):
+            at = pl.ds(pl.multiple_of(i * mem_rows, mem_rows), mem_rows)
+
+            def inner(tile, carry):
+                kv[dst, at, cols(tile)] = mm(mem[at, :], weight(piece, tile)).astype(LOW)
+                return carry
+
+            return lax.fori_loop(0, 3, inner, carry)
+
+        lax.fori_loop(0, images, body, 0)
+
+    def add_branch(src, piece, base):
+        def body(tile, carry):
+            wide[0, :, cols(tile)] = base(cols(tile)) + mm(acts[src], weight(piece, tile))
+            return carry
+
+        lax.fori_loop(0, 3, body, 0)
+
+    def normalize(which, low_dst):
+        def body(i, carry):
+            at = image(i)
+            gain, shift = norms[pl.ds(2 * which, 1), :], norms[pl.ds(2 * which + 1, 1), :]
+            out, normed, inverse = norm_rows(wide[0, at, :], gain, shift)
+            us[which, at, :] = normed
+            lane = lax.broadcasted_iota(jnp.int32, (QP, 128), 1)
+            inv[at, :] = jnp.where(lane == which, inverse, inv[at, :])
+            wide[1, at, :] = out
+            if low_dst is not None:
+                acts[low_dst, at, :] = out.astype(LOW)
+            return carry
+
+        lax.fori_loop(0, images, body, 0)
+
+    inv[...] = jnp.zeros_like(inv)
+    gather.ready(SO)
+    add_branch(3, SO, lambda at: tok[:, at].astype(WIDE))
+    normalize(0, 4)
+    gather.ready(CK)
+    memory_rows(CK, 0)
+    gather.ready(CV)
+    memory_rows(CV, 1)
+    save(kv, o_kv)
+    save(ps, o_ps)
+    gather.ready(CQ)
+    project_rows(acts.at[4], CQ, 5, 0.125)
+
+    def cross_image(i, carry):
+        at = image(i)
+        tokens = pl.ds(pl.multiple_of(i * mem_rows, mem_rows), mem_rows)
+        place = z * mem_rows + lax.broadcasted_iota(jnp.int32, (2 * QP, mem_rows), 1)
+        valid = place < lens[i]
+        lane = lax.broadcasted_iota(jnp.int32, (QP, 128), 1)
+        noted = jnp.zeros((QP, 128), WIDE)
+        for hp in range(PAIRS):
+            lanes = pl.ds(hp * 128, 128)
+            scores = mm_nt(two_heads(acts[5, at, lanes]), kv[0, tokens, lanes])
+            scores = jnp.where(valid, scores, -1e30)
+            top = jnp.max(scores, axis=-1, keepdims=True)
+            grown = jnp.where(valid, jnp.exp(scores - top), 0.0)
+            total = jnp.sum(grown, axis=-1, keepdims=True)
+            probs = grown.astype(LOW)
+            pc[i, hp] = probs
+            osend[i, :, lanes] = one_pair(mm(probs, kv[1, tokens, lanes])).astype(LOW)
+            for half in range(2):
+                head = 2 * hp + half
+                part = pl.ds(half * QP, QP)
+                span = slice(half * QP, half * QP + QP)
+                noted = jnp.where(lane == head, top[span], noted)
+                noted = jnp.where(lane == 64 + head, total[span], noted)
+        stats[i] = noted
+        return carry
+
+    lax.fori_loop(0, images, cross_image, 0)
+    pushed = []
+
+    def pass_on(src, dst, kind, r):
+        one = pltpu.make_async_remote_copy(
+            src, dst, zsend.at[kind, r - 1], zrecv.at[kind, r - 1],
+            device_id=(d, others[r - 1]), device_id_type=MESH,
+        )
+        one.start()
+        pushed.append(one)
+
+    def taken(ref, kind, r):
+        pltpu.make_async_remote_copy(
+            ref, ref, zsend.at[kind, r - 1], zrecv.at[kind, r - 1],
+            device_id=(d, others[r - 1]), device_id_type=MESH,
+        ).wait_recv()
+
+    for r in range(1, 4):
+        pass_on(osend.at[others[r - 1]], orecv.at[r - 1], 0, r)
+        pass_on(stats.at[others[r - 1]], srecv.at[r - 1], 1, r)
+    save(pc, o_pc)
+    gather.ready(CO)
+    for r in range(1, 4):
+        taken(orecv.at[r - 1], 0, r)
+        taken(srecv.at[r - 1], 1, r)
+    noted = [stats[z], srecv[0], srecv[1], srecv[2]]
+    top = functools.reduce(jnp.maximum, noted)
+    scale = [jnp.exp(one - top) for one in noted]
+    total = sum(s * pltpu.roll(one, 64, 1) for s, one in zip(scale, noted))
+    shrink = 1.0 / total
+    lane = lax.broadcasted_iota(jnp.int32, (QP, 128), 1)
+    fst[z] = jnp.where(lane < 64, top, pltpu.roll(shrink, 64, 1))
+    lower = low_lanes((QP, 128))
+    mine = image(z)
+    for hp in range(PAIRS):
+        lanes = pl.ds(hp * 128, 128)
+        joined = jnp.zeros((QP, 128), WIDE)
+        for r in range(4):
+            share = scale[r] * shrink
+            spread = jnp.where(lower, share[:, 2 * hp : 2 * hp + 1], share[:, 2 * hp + 1 : 2 * hp + 2])
+            part = osend[z, :, lanes] if r == 0 else orecv[r - 1, :, lanes]
+            joined = joined + spread * part.astype(WIDE)
+        acts[6, mine, lanes] = joined.astype(LOW)
+    for r in range(1, 4):
+        pass_on(acts.at[6, mine], acts.at[6, mine], 2, r)
+        pass_on(fst.at[z], fst.at[z], 3, r)
+    for r in range(1, 4):
+        back = lax.rem(z + 4 - r, 4)
+        taken(acts.at[6, image(back)], 2, r)
+        taken(fst.at[back], 3, r)
+    for i in range(images):
+        final = fst[i]
+        wst[i] = jnp.exp(stats[i] - final) * pltpu.roll(final, 64, 1)
+    save(wst, o_wst)
+    add_branch(6, CO, lambda at: wide[1, :, at])
+    normalize(1, 7)
+    save(acts, o_acts)
+
+    def expand(block):
+        def body(tile, carry):
+            pre = mm(acts[7], full[pl.ds((EX + block) * D, D), cols(tile)])
+            root = 0.7978845608028654
+            square = pre * pre
+            bend = jnp.tanh(root * (pre + 0.044715 * (pre * square)))
+            half = 0.5 * (1.0 + bend)
+            slope = half + (0.5 * root) * pre * (1.0 - bend * bend) * (1.0 + 0.134145 * square)
+            at = pl.ds(pl.multiple_of(block * D + tile * 256, 256), 256)
+            ffn[0, :, at] = (pre * half).astype(LOW)
+            ffn[1, :, at] = slope.astype(LOW)
+            return carry
+
+        lax.fori_loop(0, 3, body, 0)
+
+    for block in range(4):
+        gather.ready(EX + block)
+        expand(block)
+    save(ffn, o_ffn)
+    for block in range(4):
+        gather.ready(CT + block)
+    save(full, o_full)
+
+    def contract(tile, carry):
+        wide[0, :, cols(tile)] = wide[1, :, cols(tile)] + mm(
+            ffn[0], full[pl.ds(CT * D, FF), cols(tile)]
+        )
+        return carry
+
+    lax.fori_loop(0, 3, contract, 0)
+    normalize(2, None)
+    save(wide.at[1], o_result)
+    save(us, o_us)
+    save(inv, o_inv)
+    for one in pushed:
+        one.wait_send()
+    gather.close()
+    for one in kept:
+        one.wait()
+
+
+def forward(tok, mem, lens, norms, shards, images, queries, mem_rows):
+    rows = images * QP
+    shape = jax.ShapeDtypeStruct
+    tokens = images * mem_rows
+    outs = (
+        shape((rows, D), WIDE),
+        shape((PIECES * D, D), LOW),
+        shape((8, rows, D), LOW),
+        shape((2, rows, FF), LOW),
+        shape((3, rows, D), WIDE),
+        shape((rows, 128), WIDE),
+        shape((2, tokens, D), LOW),
+        shape((images, PAIRS, 2 * QP, mem_rows), LOW),
+        shape((images, PAIRS, 2 * QP, QP), LOW),
+        shape((images, QP, 128), WIDE),
+    )
+    dma = pltpu.SemaphoreType.DMA
+    return pl.pallas_call(
+        functools.partial(forward_kernel, images, queries, mem_rows),
+        out_shape=outs,
+        in_specs=[INNER, INNER, SCALAR, INNER] + [ANY] * 10,
+        out_specs=[ANY] * len(outs),
+        scratch_shapes=[
+            *[pltpu.VMEM(one.shape, one.dtype) for one in outs[1:]],
+            pltpu.VMEM((2, rows, D), WIDE),
+            pltpu.VMEM((images, QP, 128), WIDE),
+            pltpu.VMEM((images, QP, D), LOW),
+            pltpu.VMEM((3, QP, D), LOW),
+            pltpu.VMEM((3, QP, 128), WIDE),
+            pltpu.VMEM((images, QP, 128), WIDE),
+            dma((PIECES,)),
+            dma((PIECES, 7)),
+            dma((PIECES, 7)),
+            dma((4, 3)),
+            dma((4, 3)),
+            dma((12,)),
+        ],
+        compiler_params=pltpu.CompilerParams(
+            collective_id=0, has_side_effects=True, vmem_limit_bytes=VMEM_BYTES
+        ),
+        name="forward",
+    )(tok, mem, lens, norms, *(shards[place] for place in (0, 1, 2, 3, 5, 6, 4, 7, 8, 9)))
+
+
+def fused_on_device(
+    inputs,
+    memory,
+    lengths,
+    self_query,
+    self_key,
+    self_value,
+    self_out,
+    cross_query,
+    cross_key,
+    cross_value,
+    cross_out,
+    expand_weight,
+    contract_weight,
+    gain_one,
+    shift_one,
+    gain_two,
+    shift_two,
+    gain_three,
+    shift_three,
+    cotangent,
+):
+    images, queries, width = inputs.shape
+    mem_rows = memory.shape[1]
+    norms = jnp.stack([gain_one, shift_one, gain_two, shift_two, gain_three, shift_three, gain_one, gain_one])
+    shards = (self_query, self_key, self_value, self_out, cross_query, cross_key, cross_value, cross_out, expand_weight, contract_weight)
+
+    def padded(values):
+        wider = jnp.pad(values, ((0, 0), (0, QP - queries), (0, 0)))
+        return wider.reshape(images * QP, width)
+
+    def cut(values):
+        return values.reshape(images, QP, width)[:, :queries]
+
+    tokens = padded(inputs)
+    memory_flat = memory.reshape(images * mem_rows, width)
+    result, full, acts, ffn, us, inv, kv, pc, ps, wst = forward(
+        tokens, memory_flat, lengths, norms, shards, images, queries, mem_rows
+    )
+    incoming = padded(cotangent).astype(WIDE)
+    square = [full[place * D : (place + 1) * D] for place in range(8)]
+    expand_full = jnp.concatenate([full[(EX + j) * D : (EX + j + 1) * D] for j in range(4)], axis=1)
+    contract_full = full[CT * D :]
+    (sq, sk, sv, self_attn, first_low, cq, cross_attn, second_low) = [acts[place] for place in range(8)]
+    cross_probs = pc.reshape(images, H, QP, mem_rows).astype(WIDE)
+    cross_probs = cross_probs * wst[:, :, :H].transpose(0, 2, 1)[..., None]
+    self_probs = ps.reshape(images, H, QP, QP).astype(WIDE)
+
+    def scattered(part, axes="dp"):
+        return lax.psum_scatter(part, axes, scatter_dimension=0, tiled=True).astype(WIDE)
+
+    def joined(values):
+        return values.reshape(-1, width)
+
+    def heads(values):
+        return heads_of(values, images)
+
+    grad_three, gain_three_part, shift_three_part = norm_backward(incoming, us[2], inv[:, 2:3], gain_three)
+    grad_ffn = grad_three.astype(LOW)
+    contract_grad = scattered(weight_grad(ffn[0], grad_ffn).astype(LOW))
+    grad_pre = (ffn[1].astype(WIDE) * back_project(grad_ffn, contract_full)).astype(LOW)
+    expand_grad = scattered(weight_grad(second_low, grad_pre).astype(LOW))
+    grad_second = grad_three + back_project(grad_pre, expand_full)
+    grad_two, gain_two_part, shift_two_part = norm_backward(grad_second, us[1], inv[:, 1:2], gain_two)
+    grad_cross = grad_two.astype(LOW)
+    cout_part = weight_grad(cross_attn, grad_cross)
+    grad_cattn = heads(back_project(grad_cross, square[CO]).astype(LOW))
+    cross_k, cross_v = heads(kv[0]), heads(kv[1])
+    part_cquery, grad_ckey, grad_cvalue = attention_backward(
+        cross_probs, heads(cross_attn), grad_cattn, heads(cq), cross_k, cross_v
+    )
+    grad_cquery = lax.psum(joined(part_cquery).astype(LOW), "mem")
+    grad_ckey = joined(grad_ckey * 8.0).astype(LOW)
+    grad_cvalue = joined(grad_cvalue).astype(LOW)
+    kv_grad = scattered(
+        jnp.concatenate(
+            [weight_grad(memory_flat, grad_ckey), weight_grad(memory_flat, grad_cvalue)], axis=1
+        ).astype(LOW),
+        ("dp", "mem"),
+    )
+    memory_grad = back_project(grad_ckey, square[CK]) + back_project(grad_cvalue, square[CV])
+    cquery_part = weight_grad(first_low, grad_cquery)
+    grad_first = grad_two + back_project(grad_cquery, square[CQ])
+    grad_one, gain_one_part, shift_one_part = norm_backward(grad_first, us[0], inv[:, 0:1], gain_one)
+    grad_self = grad_one.astype(LOW)
+    out_part = weight_grad(self_attn, grad_self)
+    grad_sattn = heads(back_project(grad_self, square[SO]).astype(LOW))
+    grad_query, grad_key, grad_value = attention_backward(
+        self_probs, heads(self_attn), grad_sattn, heads(sq), heads(sk), heads(sv)
+    )
+    grad_query, grad_key, grad_value = (
+        joined(grad).astype(LOW) for grad in (grad_query, grad_key * 8.0, grad_value)
+    )
+    input_grad = (
+        grad_one
+        + back_project(grad_query, square[SQ])
+        + back_project(grad_key, square[SK])
+        + back_project(grad_value, square[SV])
+    )
+    norm_parts = jnp.stack(
+        [gain_one_part, shift_one_part, gain_two_part, shift_two_part, gain_three_part, shift_three_part], axis=1
+    )
+    rest = scattered(
+        jnp.concatenate(
+            [
+                weight_grad(tokens, grad_query),
+                weight_grad(tokens, grad_key),
+                weight_grad(tokens, grad_value),
+                out_part,
+                cquery_part,
+                cout_part,
+                jnp.pad(norm_parts, ((0, 0), (0, 122))),
+            ],
+            axis=1,
+        ).astype(LOW)
+    )
+    squares_grad = [rest[:, place * width : (place + 1) * width] for place in range(6)]
+    norms_grad = [rest[:, 6 * width + place] for place in range(6)]
+    return (
+        cut(result),
+        cut(input_grad),
+        memory_grad.reshape(memory.shape),
+        *squares_grad[:5],
+        kv_grad[:, :width],
+        kv_grad[:, width:],
+        squares_grad[5],
+        expand_grad,
+        contract_grad,
+        *norms_grad,
+    )
+
+
 def solution(mesh):
+    fused = mesh.shape["dp"] == 8 and mesh.shape["mem"] == 4
+
     rows = P("dp", None)
     image = P("dp", None, None)
     token = P("dp", "mem", None)
     both = P(("dp", "mem"), None)
     return jax.shard_map(
-        on_device,
+        fused_on_device if fused else on_device,
         mesh=mesh,
         in_specs=(image, token, P("dp"), *[rows] * 10, *[P()] * 6, image),
         out_specs=(image, image, token, *[rows] * 5, both, both, *[rows] * 3, *[P("dp")] * 6),

time: 723 us -> 572 us (0.79)
  waiting for transfers between devices: 361 us -> 181 us
  Pallas kernels: 0 us -> 145 us
  matrix products: 145 us -> 87.1 us
  blocking collectives: 34.8 us -> 0 us
  local copies, waits for them, and re-layouts: 141 us -> 112 us
    pallas_call x0 -> x1, Pallas kernels: none -> 145 us  [forward(): pl.pallas_call(functools.partial(forward_kernel, images, queries, mem_row...]
    all_gather x3 -> x0, waiting for transfers between devices: 130 us -> none  [the longest x1 60.3 us: on_device(): packed = lax.all_gather(jnp.stack(squares), 'dp', axis=1, tiled=True)]
    dot_general x31 -> x20, matrix products: 109 us -> 64.1 us  [contract(): return lax.dot_general(a, b, (dims, ((), ())), preferred_element_type=WIDE)]
    reshape x13 -> x2, local copies, waits for them, and re-layouts: 38.3 us -> 0.97 us  [heads_of(): return values.reshape(images, rows // images, H, width // H)]
    psum x2 -> x1, waiting for transfers between devices: 36.2 us -> 0.01 us  [fused_on_device(): grad_cquery = lax.psum(joined(part_cquery).astype(LOW), 'mem')]
    pmax x1 -> x0, blocking collectives: 19 us -> none  [on_device(): top = lax.pmax(jnp.max(cross_raw, axis=-1, keepdims=True), 'mem')]
    another operation x8 -> x20, local copies, waits for them, and re-layouts: 0.09 us -> 16.5 us  [the longest x6 15 us: heads_of(): return values.reshape(images, rows // images, H, width // H)]
    psum x1 -> x0, blocking collectives: 15.9 us -> none  [on_device(): total = lax.psum(jnp.sum(cross_exp, axis=-1, keepdims=True), 'mem')]
  transfers between devices with their start and end apart: 9 -> 5, of which waited for: 8 -> 4; matrix products, arithmetic and copies ran while one was open for 21% -> 23% of each run, Pallas kernels for 0% -> 0%
where the time goes in v2:
time: 572 us; the launch traced here: 561 us
  waiting for transfers between devices  181 us (32%)
  Pallas kernels  145 us (25%)
  local copies, waits for them, and re-layouts  112 us (20%)
  matrix products  87.1 us (15%)
  other arithmetic  18.3 us (3%)
  between operations  16.7 us (3%)
    pallas_call x1, Pallas kernels, forward(): pl.pallas_call(functools.partial(forward_kernel, images, queries, mem_row...  145 us
    reduce_scatter x2, waiting for transfers between devices, scattered(): lax.psum_scatter(part, axes, scatter_dimension=0, tiled=True).astype(WIDE)  109 us
    unnamed x7, waiting for transfers between devices  71.9 us
    dot_general x20, matrix products, contract(): return lax.dot_general(a, b, (dims, ((), ())), preferred_element_type=WIDE)  64.1 us
    unnamed x90, local copies, waits for them, and re-layouts  36.6 us
    another operation x6, local copies, waits for them, and re-layouts, heads_of(): return values.reshape(images, rows // images, H, width // H)  15 us
    dot_general x4, matrix products, mix_back(): jnp.einsum('bhqk,bqhe->bkhe', probs, grads, preferred_element_type=WIDE)  12.3 us
  transfers between devices with their start and end apart: 5, of which 4 were waited for; matrix products, arithmetic and copies ran while one was open for 23% of the time, Pallas kernels for 0%

profile of v2, /device:TPU:0, one launch (start us, length us, event | category | flops | bytes accessed | tf_op | source)
XLA Modules:
  0.0 561.2 jit_solution(11922674452043113646)
XLA Ops:
  13.1 145.4 %forward.1 = (f32[448,768]{1,0:T(8,128)}, bf16[12288,768]{1,0:T(8,128)(2,1)}, bf16[8,448,768]{2,1,0:T(8,128)(2,1)}, bf16[2,448,3072]{2,1,0:T(8,128)(2,1)}, f32[3...) custom-call(bf16[448,768]{1,0:T(8,128)(2,1)} %bitcast.162, ...), custom_call_target="tpu_custom_call" | custom-call | tf_op jit(solution)/shard_map/forward/pallas_call | solution.py:650
  160.8 4.3 fusion.89
  167.9 3.6 reshape_squeeze.20
  174.2 4.0 reshape_squeeze.21
  182.2 5.7 %fusion = bf16[448,3072]{1,0:T(8,128)(2,1)S(1)} fusion(bf16[12288,768]{1,0:T(8,128)(2,1)} %get-tuple-element.33, bf16[2,448,3072]{2,1,0:T(8,128)(2,1)} %get-tuple-element.32, f32[448,768]{1,0:T(8,128)S(1)} %bitcast.155, f32[448]{0:T(512)S(1)} %broadcast_multiply_fusion.4, f32[448]{0:T(512)S(1)} %div.23, f32[768]{0:T(1024)S(1)} %copy-done.28, ...), kind=kOutput, calls=%fused_computation.3 | convolution fusion | flops 2120122368 | bytes 12986368 | tf_op jit(solution)/shard_map/dot_general | solution.py:15
  194.8 4.6 fusion.88
  205.3 6.9 %copy.110 = f32[4,12,112,320]{2,3,1,0:T(8,128)} copy(bf16[4,12,112,320]{3,2,1,0:T(8,128)(2,1)} %bitcast.161) | data formatting | bytes 10321920 | tf_op jit(solution)/shard_map/convert_element_type | solution.py:721
  212.2 6.0 %multiply_convert_fusion = bf16[4,12,112,320]{2,3,1,0:T(8,128)(2,1)S(1)} fusion(f32[4,12,112,320]{2,3,1,0:T(8,128)} %copy.110, f32[4,12,112]{2,1,0:T(8,128)S(1)} %copy.116, f32[4,12,112]{2,1,0:T(8,128)S(1)} %copy.109, bf16[4,320,12,64]{1,0,3,2:T(4,128)(2,1)} %reshape_squeeze.21, bf16[4,112,12,64]{1,0,3,2:T(4,128)(2,1)S(1)} %reshape.158), kind=kOutput, calls=%fused_computation | convolution fusion | flops 227082240 | bytes 13019136 | tf_op jit(solution)/shard_map/bqhe,bkhe->bhqk/dot_general | solution.py:66
  222.2 6.1 %convert_bitcast_fusion = bf16[4,320,12,64]{1,3,2,0:T(8,128)(2,1)} fusion(f32[4,12,112,320]{2,3,1,0:T(8,128)} %copy.110, f32[4,12,112]{2,1,0:T(8,128)S(1)} %copy.109, bf16[4,112,12,64]{1,0,3,2:T(4,128)(2,1)S(1)} %reshape.158), kind=kOutput, calls=%fused_computation.26 | convolution fusion | flops 224624640 | bytes 9556992 | tf_op jit(solution)/shard_map/bhqk,bqhe->bkhe/dot_general | solution.py:61
  229.6 3.7 convert_bitcast_fusion.1
  238.1 3.5 copy.138
  244.7 4.0 fusion.32
  255.4 6.6 %convolution_convert_fusion = bf16[3072,768]{1,0:T(8,128)(2,1)} fusion(bf16[448,768]{1,0:T(8,128)(2,1)S(1)} %bitcast.170, bf16[2,448,3072]{2,1,0:T(8,128)(2,1)} %get-tuple-element.32), kind=kOutput, calls=%fused_computation.4 | convolution fusion | flops 2116288512 | bytes 8159232 | tf_op jit(solution)/shard_map/dot_general | solution.py:15
  263.9 5.4 convolution_convert_fusion.1
  280.9 3.5 fusion.40
  314.1 3.0 fusion.25
  317.2 3.0 fusion.20
  323.8 10.0 %copy.155 = bf16[768,4736]{1,0:T(8,128)(2,1)} copy(bf16[768,4736]{0,1:T(8,128)(2,1)} %pad_dynamic-update-slice_fusion) | data formatting | bytes 14548992
  337.1 3.2 fusion.60
  340.3 5.0 convolution_add_fusion
  353.5 3.7 reduce-scatter.15.cloned.1.call-done
  359.8 53.8 %reduce-scatter.11.cloned.1.call-done = bf16[384,768]{1,0:T(8,128)(2,1)} async-done(((bf16[3072,768]{1,0:T(8,128)(2,1)}), bf16[384,768]{1,0:T(8,128)(2,1)}) %reduce-scatter.11.cloned.1.call-update) | async-done | bytes 589840 | tf_op jit(solution)/shard_map/reduce_scatter | solution.py:726
  415.8 55.0 %reduce-scatter.9.cloned.1.call-done = bf16[96,3072]{1,0:T(8,128)(2,1)} async-done(((bf16[768,3072]{1,0:T(8,128)(2,1)}), bf16[96,3072]{1,0:T(8,128)(2,1)}) %reduce-scatter.9.cloned.1.call-update) | async-done | bytes 589840 | tf_op jit(solution)/shard_map/reduce_scatter | solution.py:726
  472.9 68.2 %reduce-scatter.13.cloned.1.call-done = bf16[96,4736]{1,0:T(8,128)(2,1)} async-done(((bf16[768,4736]{1,0:T(8,128)(2,1)}), bf16[96,4736]{1,0:T(8,128)(2,1)}) %reduce-scatter.13.cloned.1.call-update) | async-done | bytes 909328
  (189 shorter events, 126.3 us)
Async XLA Ops:
  8.0 272.9 %all-reduce.5.cloned.1.call-start = ((), (), s32[]{:S(2)}) async-start(), calls=%async_computation.4 | async-start | bytes 1572864 | tf_op jit(solution)/shard_map/psum | solution.py:748
  8.8 2.4 copy-start.29
  8.8 2.5 copy-start.26
  11.1 147.4 %copy-start.8 = (f32[4,112,768]{2,1,0:T(8,128)}, f32[4,112,768]{2,1,0:T(8,128)S(1)}, u32[]{:S(2)}) copy-start(f32[4,112,768]{2,1,0:T(8,128)S(1)} %get-tuple-element.134) | copy-start | bytes 4128772
  13.1 145.5 %copy-start.28 = (f32[768]{0:T(1024)S(1)}, f32[768]{0:T(1024)}, u32[]{:S(2)}) copy-start(f32[768]{0:T(1024)} %param.37) | copy-start | bytes 9220
  178.2 3.6 copy-start.2
  178.2 4.0 copy-start.9
  187.8 2.8 copy-start.35
  212.2 6.0 %copy-start.1 = (bf16[4,320,12,64]{1,0,3,2:T(4,128)(2,1)S(1)}, bf16[4,320,12,64]{1,0,3,2:T(4,128)(2,1)}, u32[]{:S(2)}) copy-start(bf16[4,320,12,64]{1,0,3,2:T(4,128)(2,1)} %reshape_squeeze.20) | copy-start | bytes 5898244
  222.2 6.2 %copy-start.18 = (bf16[1,448,768]{2,1,0:T(8,128)(2,1)S(1)}, bf16[1,448,768]{2,1,0:T(8,128)(2,1)}, u32[]{:S(2)}) copy-start(bf16[1,448,768]{2,1,0:T(8,128)(2,1)} %get-tuple-element.113) | copy-start | bytes 2064388
  222.2 135.0 %reduce-scatter.15.cloned.1.call-start = ((), (), s32[]{:S(2)}) async-start(), calls=%async_computation.8 | async-start | bytes 2433024
  244.6 4.0 copy-start.20
  244.6 4.0 copy-start.23
  253.0 160.6 %reduce-scatter.11.cloned.1.call-start = ((), (), s32[]{:S(2)}) async-start(), calls=%async_computation.6 | async-start | bytes 5308416 | tf_op jit(solution)/shard_map/reduce_scatter | solution.py:726
  262.1 208.6 %reduce-scatter.9.cloned.1.call-start = ((), (), s32[]{:S(2)}) async-start(), calls=%async_computation.5 | async-start | bytes 5308416 | tf_op jit(solution)/shard_map/reduce_scatter | solution.py:726
  269.3 271.7 %reduce-scatter.13.cloned.1.call-start = ((), (), s32[]{:S(2)}) async-start(), calls=%async_computation.7 | async-start | bytes 8183808
  272.3 2.5 copy-start.17
  291.7 2.8 copy-start.3
  300.8 4.1 copy-start.10
  307.5 3.0 copy-start.11
  307.5 3.0 copy-start.14
  314.1 3.0 copy-start.34
  317.2 3.0 copy-start.25
  337.1 3.2 copy-start.22
  (18 other events, 34.1 us)
Sparse Core Ops, SparseCore 0:
  222.3 48.9 all-reduce.4
Sparse Core Ops, SparseCore 1:
  253.1 104.0 reduce-scatter.14
  360.8 52.7 reduce-scatter.10
  416.9 53.7 reduce-scatter.8
  474.6 66.4 reduce-scatter.12

commit v3 on v2

--- a/solution.py
+++ b/solution.py
@@ -674,6 +674,565 @@
     )(tok, mem, lens, norms, *(shards[place] for place in (0, 1, 2, 3, 5, 6, 4, 7, 8, 9)))
 
 
+def rows_of_image(i):
+    return pl.ds(pl.multiple_of(i * QP, QP), QP)
+
+
+def cols_of_tile(tile):
+    return pl.ds(pl.multiple_of(tile * 256, 256), 256)
+
+
+class Reduce:
+    def __init__(self, where, turn, grad, core_in, chip_in, core_sems, chip_sems):
+        self.where, self.turn = where, turn
+        self.grad, self.core_in, self.chip_in = grad, core_in, chip_in
+        self.core_sems, self.chip_sems = core_sems, chip_sems
+        self.sent = []
+        d, other, beside, above, across = where
+        self.c = lax.rem(d, 2)
+        self.z = lax.axis_index("mem")
+
+    def copy(self, src, dst, sems, place, target):
+        return pltpu.make_async_remote_copy(
+            src, dst, sems.at[0, self.turn, place], sems.at[1, self.turn, place],
+            device_id=(target, self.z), device_id_type=MESH,
+        )
+
+    def core_stage(self):
+        one = self.copy(self.grad.at[1 - self.c], self.core_in, self.core_sems, 0, self.where[1])
+        one.start()
+        self.sent.append(one)
+
+    def chip_stage(self):
+        self.copy(self.core_in, self.core_in, self.core_sems, 0, self.where[1]).wait_recv()
+        for chip in range(4):
+            both = self.grad[self.c, chip].astype(WIDE) + self.core_in[chip].astype(WIDE)
+            self.grad[self.c, chip] = both.astype(LOW)
+        for place, target in enumerate(self.where[2:]):
+            one = self.copy(
+                self.grad.at[self.c, target // 2], self.chip_in.at[place], self.chip_sems, place, target
+            )
+            one.start()
+            self.sent.append(one)
+
+    def total(self):
+        own = self.grad[self.c, self.where[0] // 2].astype(WIDE)
+        for place, target in enumerate(self.where[2:]):
+            self.copy(
+                self.chip_in.at[place], self.chip_in.at[place], self.chip_sems, place, target
+            ).wait_recv()
+            own = own + self.chip_in[place].astype(WIDE)
+        return own
+
+    def settle(self):
+        for one in self.sent:
+            one.wait_send()
+        self.sent = []
+
+
+def backward_kernel(images, queries, mem_rows, *refs):
+    (
+        h_norms, h_cot, h_tok, h_mem, h_full, h_acts, h_ffn, h_us, h_inv, h_kv, h_pc, h_ps, h_wst,
+    ) = refs[:13]
+    (o_expand, o_contract, o_rest, o_keys, o_mem, o_in, o_norms) = refs[13:20]
+    (
+        norms, cot, tok, mem, slots, acts, ffn, us, inv, kv, pc, ps, wst, wide, grads, nsum, nin,
+        zsend, zin, mout,
+        g_expand, g_contract, g_rest, c_expand, c_contract, c_rest, c_keys,
+        t_expand, t_contract, t_rest, t_keys, f_expand, f_contract, f_rest, k_out, k_in,
+        load, slot_sems, pc_sems, mout_sems, core_sems, chip_sems, fin_sems, local_sems, ksems, zsems, nsems,
+    ) = refs[20:]
+    z = lax.axis_index("mem")
+    d = lax.axis_index("dp")
+    where = places()
+    q = lax.rem(z, 2)
+    zp = z + 1 - 2 * q
+    others = [lax.rem(z + r, 4) for r in range(1, 4)]
+    dpeers = [lax.rem(d + r, 8) for r in range(1, 8)]
+
+    loads = {}
+    waited = set()
+
+    def fetch(name, src, dst):
+        one = pltpu.make_async_copy(src, dst, load.at[len(loads)])
+        one.start()
+        loads[name] = one
+
+    order = [CT, CT + 1, CT + 2, CT + 3, EX, EX + 1, EX + 2, EX + 3, CO, CK, CV, CQ, SO, SQ, SK, SV]
+    depth = 4
+
+    def slot_copy(turn):
+        return pltpu.make_async_copy(
+            h_full.at[pl.ds(order[turn] * D, D)], slots.at[turn % depth], slot_sems.at[turn % depth]
+        )
+
+    def prefetch(turn):
+        if turn < len(order):
+            slot_copy(turn).start()
+
+    fetch("norms", h_norms, norms)
+    fetch("cot", h_cot, cot)
+    fetch("inv", h_inv, inv)
+    fetch("u3", h_us.at[2], us.at[0])
+    for turn in range(depth):
+        prefetch(turn)
+    fetch("gp", h_ffn.at[1], ffn.at[1])
+    fetch("act", h_ffn.at[0], ffn.at[0])
+    fetch("acts", h_acts, acts)
+    fetch("u2", h_us.at[1], us.at[1])
+    fetch("kv", h_kv, kv)
+    fetch("wst", h_wst, wst)
+    fetch("ps", h_ps, ps)
+    fetch("mem", h_mem, mem)
+    fetch("tok", h_tok, tok)
+
+    def have(name):
+        if name not in waited:
+            waited.add(name)
+            loads[name].wait()
+
+    def pc_copy(turn):
+        i = lax.rem(z + turn + 1, 4)
+        return pltpu.make_async_copy(h_pc.at[i], pc.at[turn % 2], pc_sems.at[turn % 2])
+
+    pc_copy(0).start()
+    pc_copy(1).start()
+    greet([(peer, z) for peer in dpeers] + [(d, other) for other in others])
+
+    nsum[...] = jnp.zeros_like(nsum)
+
+    def norm_back(which, incoming, slot, low_dst):
+        def body(i, carry):
+            at = rows_of_image(i)
+            above = incoming(at)
+            unit = us[slot, at, :]
+            inverse = inv[at, which : which + 1]
+            scaled = above * norms[2 * which : 2 * which + 1, :]
+            first = jnp.mean(scaled, axis=-1, keepdims=True)
+            second = jnp.mean(scaled * unit, axis=-1, keepdims=True)
+            grad = inverse * (scaled - first - unit * second)
+            wide[0, at, :] = grad
+            grads[low_dst, at, :] = grad.astype(LOW)
+            row = 2 * which
+            nsum[row : row + 1, :] += jnp.sum(above * unit, axis=0, keepdims=True)
+            nsum[row + 1 : row + 2, :] += jnp.sum(above, axis=0, keepdims=True)
+            return carry
+
+        lax.fori_loop(0, images, body, 0)
+
+    turn_of = {piece: turn for turn, piece in enumerate(order)}
+
+    def slot(piece):
+        turn = turn_of[piece]
+        slot_copy(turn).wait()
+        return slots.at[turn % depth]
+
+    def freed(piece):
+        prefetch(turn_of[piece] + depth)
+
+    for name in ("norms", "cot", "inv", "u3"):
+        have(name)
+    norm_back(2, lambda at: cot[at, :].astype(WIDE), 0, 0)
+    fetch("u1", h_us.at[0], us.at[0])
+    have("gp")
+    for block in range(4):
+        weight = slot(CT + block)
+
+        def body(tile, carry):
+            at = pl.ds(pl.multiple_of(block * D + tile * 256, 256), 256)
+            back = mm_nt(grads[0], weight[cols_of_tile(tile), :])
+            ffn[1, :, at] = (back * ffn[1, :, at].astype(WIDE)).astype(LOW)
+            return carry
+
+        lax.fori_loop(0, 3, body, 0)
+        freed(CT + block)
+
+    def reduce_at(place, grad, core_in, chip_in):
+        return Reduce(where, place, grad, core_in, chip_in, core_sems, chip_sems)
+
+    have("acts")
+    r_expand = reduce_at(0, g_expand, c_expand, t_expand)
+
+    def expand_part(tile, carry):
+        at = pl.ds(pl.multiple_of(q * 1536 + tile * 256, 256), 256)
+        out = mm_tn(acts[7], ffn[1, :, at]).astype(LOW)
+        for e in range(8):
+            g_expand[e % 2, e // 2, :, cols_of_tile(tile)] = out[96 * e : 96 * e + 96]
+        return carry
+
+    lax.fori_loop(0, 6, expand_part, 0)
+    r_expand.core_stage()
+    have("act")
+    r_contract = reduce_at(1, g_contract, c_contract, t_contract)
+
+    def contract_part(e, carry):
+        at = pl.ds(pl.multiple_of(e * 384, 384), 384)
+        half = pl.ds(pl.multiple_of(q * 384, 384), 384)
+        g_contract[lax.rem(e, 2), e // 2] = mm_tn(ffn[0, :, at], grads[0, :, half]).astype(LOW)
+        return carry
+
+    lax.fori_loop(0, 8, contract_part, 0)
+    r_contract.core_stage()
+    r_expand.chip_stage()
+    for block in range(4):
+        weight = slot(EX + block)
+
+        def body(tile, carry):
+            at = cols_of_tile(tile)
+            back = mm_nt(ffn[1, :, pl.ds(block * D, D)], weight[at, :])
+            wide[0, :, at] = wide[0, :, at] + back
+            return carry
+
+        lax.fori_loop(0, 3, body, 0)
+        freed(EX + block)
+    r_contract.chip_stage()
+    have("u2")
+    norm_back(1, lambda at: wide[0, at, :], 1, 1)
+
+    def through(src, piece, dst):
+        weight = slot(piece)
+
+        def body(tile, carry):
+            grads[dst, :, cols_of_tile(tile)] = mm_nt(grads[src], weight[cols_of_tile(tile), :]).astype(LOW)
+            return carry
+
+        lax.fori_loop(0, 3, body, 0)
+        freed(piece)
+
+    through(1, CO, 0)
+    have("kv")
+    have("wst")
+    pushed = []
+
+    def across_mem(src, dst, kind, r):
+        return pltpu.make_async_remote_copy(
+            src, dst, zsems.at[0, kind, r - 1], zsems.at[1, kind, r - 1],
+            device_id=(d, others[r - 1]), device_id_type=MESH,
+        )
+
+    for turn in range(4):
+        i = lax.rem(z + turn + 1, 4)
+        pc_copy(turn).wait()
+        at = rows_of_image(i)
+        tokens = pl.ds(pl.multiple_of(i * mem_rows, mem_rows), mem_rows)
+        factors = wst[i]
+
+        def pair(hp, carry):
+            lanes = pl.ds(pl.multiple_of(hp * 128, 128), 128)
+            query = two_heads(acts[5, at, lanes])
+            above = two_heads(grads[0, at, lanes])
+            attn = acts[6, at, lanes].astype(WIDE)
+            row = jnp.sum(above.astype(WIDE) * jnp.concatenate([attn, attn], axis=0), axis=-1, keepdims=True)
+            lane = lax.broadcasted_iota(jnp.int32, (QP, 128), 1)
+            factor = jnp.concatenate(
+                [
+                    jnp.sum(jnp.where(lane == 2 * hp + half, factors, 0.0), axis=-1, keepdims=True)
+                    for half in range(2)
+                ],
+                axis=0,
+            )
+            probs = pc[turn % 2, hp].astype(WIDE) * factor
+            keys, values = kv[0, tokens, lanes], kv[1, tokens, lanes]
+            inner = mm_nt(above, values)
+            scores = (probs * (inner - row)).astype(LOW)
+            zsend[turn, :, lanes] = (one_pair(mm(scores, keys)) * 0.125).astype(LOW)
+            kv[0, tokens, lanes] = mm_tn(scores, query).astype(LOW)
+            kv[1, tokens, lanes] = mm_tn(probs.astype(LOW), above).astype(LOW)
+            return carry
+
+        lax.fori_loop(0, PAIRS, pair, 0)
+        if turn < 2:
+            pc_copy(turn + 2).start()
+        if turn < 3:
+            one = across_mem(zsend.at[turn], zin.at[turn], 0, turn + 1)
+            one.start()
+            pushed.append(one)
+
+    have("mem")
+    r_expand.settle()
+    r_keys = reduce_at(2, g_expand, c_keys, t_keys)
+    for which in range(2):
+
+        def key_part(tile, carry):
+            out = mm_tn(mem[...], kv[which, :, cols_of_tile(tile)]).astype(LOW)
+            at = pl.ds(pl.multiple_of(which * D + tile * 256, 256), 256)
+            for e in range(8):
+                g_expand[e % 2, e // 2, :, at] = out[96 * e : 96 * e + 96]
+            return carry
+
+        if which == 0:
+            final_expand = r_expand.total()
+            f_expand[...] = final_expand.astype(LOW)
+        lax.fori_loop(0, 3, key_part, 0)
+    r_keys.core_stage()
+    for r in range(1, 4):
+        across_mem(zin.at[r - 1], zin.at[r - 1], 0, r).wait_recv()
+    mine = rows_of_image(z)
+    grads[3, mine, :] = (
+        zsend[3].astype(WIDE) + zin[0].astype(WIDE) + zin[1].astype(WIDE) + zin[2].astype(WIDE)
+    ).astype(LOW)
+    for r in range(1, 4):
+        one = across_mem(grads.at[3, mine], grads.at[3, mine], 1, r)
+        one.start()
+        pushed.append(one)
+
+    def finals(fin, out, place):
+        pltpu.make_async_copy(fin, out, local_sems.at[place]).start()
+        one = pltpu.make_async_remote_copy(
+            fin, out, fin_sems.at[0, place], fin_sems.at[1, place], device_id=(d, zp), device_id_type=MESH
+        )
+        one.start()
+        return one
+
+    ended = []
+    r_keys.chip_stage()
+    key_weight, value_weight = slot(CK), slot(CV)
+    for i in range(images):
+        at = pl.ds(i * mem_rows, mem_rows)
+        if i >= 2:
+            pltpu.make_async_copy(mout.at[i % 2], o_mem.at[at], mout_sems.at[i % 2]).wait()
+
+        def body(tile, carry):
+            span = cols_of_tile(tile)
+            mout[i % 2, :, span] = mm_nt(kv[0, at, :], key_weight[span, :]) + mm_nt(
+                kv[1, at, :], value_weight[span, :]
+            )
+            return carry
+
+        lax.fori_loop(0, 3, body, 0)
+        pltpu.make_async_copy(mout.at[i % 2], o_mem.at[at], mout_sems.at[i % 2]).start()
+    freed(CK)
+    freed(CV)
+    for r in range(1, 4):
+        back = lax.rem(z + 4 - r, 4)
+        across_mem(grads.at[3, rows_of_image(back)], grads.at[3, rows_of_image(back)], 1, r).wait_recv()
+    ended.append(finals(f_expand, o_expand.at[q], 0))
+    f_contract[...] = r_contract.total().astype(LOW)
+    ended.append(finals(f_contract, o_contract.at[q], 1))
+
+    def add_back(src, piece):
+        weight = slot(piece)
+
+        def body(tile, carry):
+            span = cols_of_tile(tile)
+            wide[0, :, span] = wide[0, :, span] + mm_nt(src(), weight[span, :])
+            return carry
+
+        lax.fori_loop(0, 3, body, 0)
+        freed(piece)
+
+    add_back(lambda: grads[3], CQ)
+    have("u1")
+    norm_back(0, lambda at: wide[0, at, :], 0, 2)
+    for r in range(1, 8):
+        one = pltpu.make_async_remote_copy(
+            nsum, nin.at[r - 1], nsems.at[0, r - 1], nsems.at[1, r - 1],
+            device_id=(dpeers[r - 1], z), device_id_type=MESH,
+        )
+        one.start()
+        pushed.append(one)
+    have("tok")
+
+    def rest_part(turn, lefts, rights):
+        reducer = reduce_at(3 + turn, g_rest.at[turn], c_rest.at[turn], t_rest.at[turn])
+
+        def work(left, right):
+            def body(tile, carry):
+                out = mm_tn(left(), right(cols_of_tile(tile))).astype(LOW)
+                for e in range(8):
+                    g_rest[turn, e % 2, e // 2, :, cols_of_tile(tile)] = out[96 * e : 96 * e + 96]
+                return carry
+
+            lax.fori_loop(0, 3, body, 0)
+
+        @pl.when(q == 0)
+        def _():
+            work(lefts[0], rights[0])
+
+        @pl.when(q == 1)
+        def _():
+            work(lefts[1], rights[1])
+
+        reducer.core_stage()
+        return reducer
+
+    r_first = rest_part(
+        0,
+        (lambda: acts[6], lambda: acts[4]),
+        (lambda at: grads[1, :, at], lambda at: grads[3, :, at]),
+    )
+    through(2, SO, 0)
+    have("ps")
+    r_first.chip_stage()
+
+    def self_image(i, carry):
+        at = rows_of_image(i)
+        for hp in range(PAIRS):
+            lanes = pl.ds(hp * 128, 128)
+            query = two_heads(acts[0, at, lanes])
+            above = two_heads(grads[0, at, lanes])
+            attn = acts[3, at, lanes].astype(WIDE)
+            row = jnp.sum(above.astype(WIDE) * jnp.concatenate([attn, attn], axis=0), axis=-1, keepdims=True)
+            probs = ps[i, hp]
+            keys, values = acts[1, at, lanes], acts[2, at, lanes]
+            inner = mm_nt(above, values)
+            scores = (probs.astype(WIDE) * (inner - row)).astype(LOW)
+            acts[0, at, lanes] = (one_pair(mm(scores, keys)) * 0.125).astype(LOW)
+            acts[1, at, lanes] = mm_tn(scores, query).astype(LOW)
+            acts[2, at, lanes] = mm_tn(probs, above).astype(LOW)
+        return carry
+
+    lax.fori_loop(0, images, self_image, 0)
+    r_second = rest_part(
+        1,
+        (lambda: acts[3], lambda: tok[...]),
+        (lambda at: grads[2, :, at], lambda at: acts[0, :, at]),
+    )
+    r_third = rest_part(
+        2,
+        (lambda: tok[...], lambda: tok[...]),
+        (lambda at: acts[1, :, at], lambda at: acts[2, :, at]),
+    )
+    r_second.chip_stage()
+    r_third.chip_stage()
+    quarter = 24
+    keys_total = r_keys.total()
+    for part in range(4):
+        k_out[part] = keys_total[quarter * part : quarter * part + quarter].astype(LOW)
+    for r in range(1, 4):
+        one = pltpu.make_async_remote_copy(
+            k_out.at[others[r - 1]], k_in.at[r - 1], ksems.at[0, r - 1], ksems.at[1, r - 1],
+            device_id=(d, others[r - 1]), device_id_type=MESH,
+        )
+        one.start()
+        pushed.append(one)
+    f_rest[0] = r_first.total().astype(LOW)
+    ended.append(finals(f_rest.at[0], o_rest.at[0, q], 2))
+    add_back(lambda: acts[0], SQ)
+    add_back(lambda: acts[1], SK)
+    add_back(lambda: acts[2], SV)
+    pltpu.make_async_copy(wide.at[0], o_in, load.at[15]).start()
+    f_rest[1] = r_second.total().astype(LOW)
+    ended.append(finals(f_rest.at[1], o_rest.at[1, q], 3))
+    f_rest[2] = r_third.total().astype(LOW)
+    ended.append(finals(f_rest.at[2], o_rest.at[2, q], 4))
+    sums = nsum[...]
+    for r in range(1, 8):
+        pltpu.make_async_remote_copy(
+            nsum, nin.at[r - 1], nsems.at[0, r - 1], nsems.at[1, r - 1],
+            device_id=(dpeers[r - 1], z), device_id_type=MESH,
+        ).wait_recv()
+        sums = sums + nin[r - 1]
+    o_norms[...] = sums
+    total = k_out[z].astype(WIDE)
+    for r in range(1, 4):
+        pltpu.make_async_remote_copy(
+            k_in.at[r - 1], k_in.at[r - 1], ksems.at[0, r - 1], ksems.at[1, r - 1],
+            device_id=(d, others[r - 1]), device_id_type=MESH,
+        ).wait_recv()
+        total = total + k_in[r - 1].astype(WIDE)
+    o_keys[...] = total
+    for i in range(2, 4):
+        at = pl.ds(i * mem_rows, mem_rows)
+        pltpu.make_async_copy(mout.at[i % 2], o_mem.at[at], mout_sems.at[i % 2]).wait()
+    pltpu.make_async_copy(wide.at[0], o_in, load.at[15]).wait()
+    fins = (f_expand, f_contract, f_rest.at[0], f_rest.at[1], f_rest.at[2])
+    outs = (
+        (o_expand.at[q], o_expand.at[1 - q]),
+        (o_contract.at[q], o_contract.at[1 - q]),
+        (o_rest.at[0, q], o_rest.at[0, 1 - q]),
+        (o_rest.at[1, q], o_rest.at[1, 1 - q]),
+        (o_rest.at[2, q], o_rest.at[2, 1 - q]),
+    )
+    for place, (fin, (out, theirs)) in enumerate(zip(fins, outs)):
+        pltpu.make_async_copy(fin, out, local_sems.at[place]).wait()
+        ended[place].wait_send()
+        pltpu.make_async_remote_copy(
+            fin, theirs, fin_sems.at[0, place], fin_sems.at[1, place], device_id=(d, zp), device_id_type=MESH
+        ).wait_recv()
+    for one in pushed:
+        one.wait_send()
+    for reducer in (r_contract, r_keys, r_first, r_second, r_third):
+        reducer.settle()
+
+
+def backward(norms, cot, tok, mem, saved, images, queries, mem_rows):
+    full, acts, ffn, us, inv, kv, pc, ps, wst = saved
+    rows = images * QP
+    tokens = images * mem_rows
+    shape = jax.ShapeDtypeStruct
+    outs = (
+        shape((2, 96, 1536), LOW),
+        shape((2, 384, 384), LOW),
+        shape((3, 2, 96, D), LOW),
+        shape((24, 1536), WIDE),
+        shape((tokens, D), WIDE),
+        shape((rows, D), WIDE),
+        shape((8, D), WIDE),
+    )
+    dma = pltpu.SemaphoreType.DMA
+    vmem = pltpu.VMEM
+    return pl.pallas_call(
+        functools.partial(backward_kernel, images, queries, mem_rows),
+        out_shape=outs,
+        in_specs=[ANY] * 13,
+        out_specs=[ANY] * 3 + [INNER] + [ANY] * 2 + [INNER],
+        scratch_shapes=[
+            vmem((8, D), WIDE),
+            vmem((rows, D), LOW),
+            vmem((rows, D), LOW),
+            vmem((tokens, D), LOW),
+            vmem((4, D, D), LOW),
+            vmem((8, rows, D), LOW),
+            vmem((2, rows, FF), LOW),
+            vmem((2, rows, D), WIDE),
+            vmem((rows, 128), WIDE),
+            vmem((2, tokens, D), LOW),
+            vmem((2, PAIRS, 2 * QP, mem_rows), LOW),
+            vmem((images, PAIRS, 2 * QP, QP), LOW),
+            vmem((images, QP, 128), WIDE),
+            vmem((1, rows, D), WIDE),
+            vmem((4, rows, D), LOW),
+            vmem((8, D), WIDE),
+            vmem((7, 8, D), WIDE),
+            vmem((4, QP, D), LOW),
+            vmem((3, QP, D), LOW),
+            vmem((2, mem_rows, D), WIDE),
+            vmem((2, 4, 96, 1536), LOW),
+            vmem((2, 4, 384, 384), LOW),
+            vmem((3, 2, 4, 96, D), LOW),
+            vmem((4, 96, 1536), LOW),
+            vmem((4, 384, 384), LOW),
+            vmem((3, 4, 96, D), LOW),
+            vmem((4, 96, 1536), LOW),
+            vmem((3, 96, 1536), LOW),
+            vmem((3, 384, 384), LOW),
+            vmem((3, 3, 96, D), LOW),
+            vmem((3, 96, 1536), LOW),
+            vmem((96, 1536), LOW),
+            vmem((384, 384), LOW),
+            vmem((3, 96, D), LOW),
+            vmem((4, 24, 1536), LOW),
+            vmem((3, 24, 1536), LOW),
+            dma((16,)),
+            dma((4,)),
+            dma((2,)),
+            dma((2,)),
+            dma((2, 6, 1)),
+            dma((2, 6, 3)),
+            dma((2, 5)),
+            dma((5,)),
+            dma((2, 3)),
+            dma((2, 2, 3)),
+            dma((2, 7)),
+        ],
+        compiler_params=pltpu.CompilerParams(
+            collective_id=1, has_side_effects=True, vmem_limit_bytes=VMEM_BYTES
+        ),
+        name="backward",
+    )(norms, cot, tok, mem, *saved)
+
+
 def fused_on_device(
     inputs,
     memory,
@@ -713,96 +1272,28 @@
     result, full, acts, ffn, us, inv, kv, pc, ps, wst = forward(
         tokens, memory_flat, lengths, norms, shards, images, queries, mem_rows
     )
-    incoming = padded(cotangent).astype(WIDE)
-    square = [full[place * D : (place + 1) * D] for place in range(8)]
-    expand_full = jnp.concatenate([full[(EX + j) * D : (EX + j + 1) * D] for j in range(4)], axis=1)
-    contract_full = full[CT * D :]
-    (sq, sk, sv, self_attn, first_low, cq, cross_attn, second_low) = [acts[place] for place in range(8)]
-    cross_probs = pc.reshape(images, H, QP, mem_rows).astype(WIDE)
-    cross_probs = cross_probs * wst[:, :, :H].transpose(0, 2, 1)[..., None]
-    self_probs = ps.reshape(images, H, QP, QP).astype(WIDE)
-
-    def scattered(part, axes="dp"):
-        return lax.psum_scatter(part, axes, scatter_dimension=0, tiled=True).astype(WIDE)
-
-    def joined(values):
-        return values.reshape(-1, width)
-
-    def heads(values):
-        return heads_of(values, images)
-
-    grad_three, gain_three_part, shift_three_part = norm_backward(incoming, us[2], inv[:, 2:3], gain_three)
-    grad_ffn = grad_three.astype(LOW)
-    contract_grad = scattered(weight_grad(ffn[0], grad_ffn).astype(LOW))
-    grad_pre = (ffn[1].astype(WIDE) * back_project(grad_ffn, contract_full)).astype(LOW)
-    expand_grad = scattered(weight_grad(second_low, grad_pre).astype(LOW))
-    grad_second = grad_three + back_project(grad_pre, expand_full)
-    grad_two, gain_two_part, shift_two_part = norm_backward(grad_second, us[1], inv[:, 1:2], gain_two)
-    grad_cross = grad_two.astype(LOW)
-    cout_part = weight_grad(cross_attn, grad_cross)
-    grad_cattn = heads(back_project(grad_cross, square[CO]).astype(LOW))
-    cross_k, cross_v = heads(kv[0]), heads(kv[1])
-    part_cquery, grad_ckey, grad_cvalue = attention_backward(
-        cross_probs, heads(cross_attn), grad_cattn, heads(cq), cross_k, cross_v
-    )
-    grad_cquery = lax.psum(joined(part_cquery).astype(LOW), "mem")
-    grad_ckey = joined(grad_ckey * 8.0).astype(LOW)
-    grad_cvalue = joined(grad_cvalue).astype(LOW)
-    kv_grad = scattered(
-        jnp.concatenate(
-            [weight_grad(memory_flat, grad_ckey), weight_grad(memory_flat, grad_cvalue)], axis=1
-        ).astype(LOW),
-        ("dp", "mem"),
-    )
-    memory_grad = back_project(grad_ckey, square[CK]) + back_project(grad_cvalue, square[CV])
-    cquery_part = weight_grad(first_low, grad_cquery)
-    grad_first = grad_two + back_project(grad_cquery, square[CQ])
-    grad_one, gain_one_part, shift_one_part = norm_backward(grad_first, us[0], inv[:, 0:1], gain_one)
-    grad_self = grad_one.astype(LOW)
-    out_part = weight_grad(self_attn, grad_self)
-    grad_sattn = heads(back_project(grad_self, square[SO]).astype(LOW))
-    grad_query, grad_key, grad_value = attention_backward(
-        self_probs, heads(self_attn), grad_sattn, heads(sq), heads(sk), heads(sv)
-    )
-    grad_query, grad_key, grad_value = (
-        joined(grad).astype(LOW) for grad in (grad_query, grad_key * 8.0, grad_value)
-    )
-    input_grad = (
-        grad_one
-        + back_project(grad_query, square[SQ])
-        + back_project(grad_key, square[SK])
-        + back_project(grad_value, square[SV])
-    )
-    norm_parts = jnp.stack(
-        [gain_one_part, shift_one_part, gain_two_part, shift_two_part, gain_three_part, shift_three_part], axis=1
-    )
-    rest = scattered(
-        jnp.concatenate(
-            [
-                weight_grad(tokens, grad_query),
-                weight_grad(tokens, grad_key),
-                weight_grad(tokens, grad_value),
-                out_part,
-                cquery_part,
-                cout_part,
-                jnp.pad(norm_parts, ((0, 0), (0, 122))),
-            ],
-            axis=1,
-        ).astype(LOW)
-    )
-    squares_grad = [rest[:, place * width : (place + 1) * width] for place in range(6)]
-    norms_grad = [rest[:, 6 * width + place] for place in range(6)]
+    spread, contracted, rest, keys, memory_grad, input_grad, sums = backward(
+        norms, padded(cotangent), tokens, memory_flat, (full, acts, ffn, us, inv, kv, pc, ps, wst),
+        images, queries, mem_rows,
+    )
+    share = self_query.shape[0]
+    sums = lax.dynamic_slice(sums, (0, lax.axis_index("dp") * share), (8, share))
+    rest = rest.astype(WIDE)
     return (
         cut(result),
         cut(input_grad),
         memory_grad.reshape(memory.shape),
-        *squares_grad[:5],
-        kv_grad[:, :width],
-        kv_grad[:, width:],
-        squares_grad[5],
-        expand_grad,
-        contract_grad,
-        *norms_grad,
+        rest[1, 1],
+        rest[2, 0],
+        rest[2, 1],
+        rest[1, 0],
+        rest[0, 1],
+        keys[:, :width],
+        keys[:, width:],
+        rest[0, 0],
+        jnp.concatenate([spread[0], spread[1]], axis=1).astype(WIDE),
+        jnp.concatenate([contracted[0], contracted[1]], axis=1).astype(WIDE),
+        *[sums[place] for place in range(6)],
     )
 
 

time: 572 us -> 268 us (0.47); the launches traced: 561 us -> 265 us
  waiting for transfers between devices: 181 us -> 0 us
  Pallas kernels: 145 us -> 245 us
  local copies, waits for them, and re-layouts: 112 us -> 17.2 us
  matrix products: 87.1 us -> 0 us
  other arithmetic: 18.3 us -> 2.36 us
  between operations: 16.7 us -> 0.87 us
    reduce_scatter x2 -> x0, waiting for transfers between devices: 109 us -> none  [scattered(): lax.psum_scatter(part, axes, scatter_dimension=0, tiled=True).astype(WIDE)]
    pallas_call x0 -> x1, Pallas kernels: none -> 99.3 us  [backward(): pl.pallas_call(functools.partial(backward_kernel, images, queries, mem_ro...]
    dot_general x28 -> x0, matrix products: 87.1 us -> none  [the longest x20 64.1 us: contract(): return lax.dot_general(a, b, (dims, ((), ())), preferred_element_type=WIDE)]
    unnamed x7 -> x0, waiting for transfers between devices: 71.9 us -> none
    convert_element_type x19 -> x0, local copies, waits for them, and re-layouts: 38.1 us -> none  [the longest x6 9.3 us: fused_on_device(): joined(grad).astype(LOW)]
    unnamed x90 -> x27, local copies, waits for them, and re-layouts: 36.6 us -> 8.7 us
    another operation x13 -> x0, local copies, waits for them, and re-layouts: 15.1 us -> none  [the longest x6 15 us: heads_of(): return values.reshape(images, rows // images, H, width // H)]
    slice x8 -> x1, local copies, waits for them, and re-layouts: 15.3 us -> 0.66 us  [fused_on_device(): keys[:, width:]]
  transfers between devices with their start and end apart: 5 -> 0, of which waited for: 4 -> 0; matrix products, arithmetic and copies ran while one was open for 23% -> 0% of each run, Pallas kernels for 0% -> 0%
where the time goes in v3:
time: 268 us; the launch traced here: 265 us
  Pallas kernels  245 us (91%)
  local copies, waits for them, and re-layouts  17.2 us (6%)
    pallas_call x1, Pallas kernels, forward(): pl.pallas_call(functools.partial(forward_kernel, images, queries, mem_row...  145 us
    pallas_call x1, Pallas kernels, backward(): pl.pallas_call(functools.partial(backward_kernel, images, queries, mem_ro...  99.3 us
    unnamed x27, local copies, waits for them, and re-layouts  8.7 us

profile of v3, /device:TPU:0, one launch (start us, length us, event | category | flops | bytes accessed | tf_op | source)
XLA Modules:
  0.0 265.3 jit_solution(14526570786167153744)
XLA Ops:
  0.7 1.2 copy.45
  1.9 0.9 pad.7.clone
  2.8 0.0 copy-done.8
  2.9 0.7 stack.29.refs_3_.refs_0_
  3.6 145.5 %forward.1 = (f32[448,768]{1,0:T(8,128)}, bf16[12288,768]{1,0:T(8,128)(2,1)}, bf16[8,448,768]{2,1,0:T(8,128)(2,1)}, bf16[2,448,3072]{2,1,0:T(8,128)(2,1)}, f32[3...) custom-call(bf16[448,768]{1,0:T(8,128)(2,1)} %bitcast.40, ...), custom_call_target="tpu_custom_call" | custom-call | tf_op jit(solution)/shard_map/forward/pallas_call | solution.py:650
  149.0 1.4 slice.80
  150.4 0.0 copy-start.1
  150.4 1.5 copy.43
  151.9 0.1 copy.46
  152.0 0.9 pad.8.clone
  152.9 99.3 %backward.1 = (bf16[2,96,1536]{2,1,0:T(8,128)(2,1)}, bf16[2,384,384]{2,1,0:T(8,128)(2,1)}, bf16[3,2,96,768]{3,2,1,0:T(8,128)(2,1)}, f32[24,1536]{1,0:T(8,128)}, ...) custom-call(f32[8,768]{1,0:T(8,128)} %stack.29.refs_3_.refs_0_, bf16[448,768]{1,0:T(8,128)(2,1)} %bitcast.43, ...), custom_call_target="tpu_custom_call" | custom-call | tf_op jit(solution)/shard_map/backward/pallas_call | solution.py:1175
  252.2 1.4 slice.81
  253.7 1.5 copy.44
  255.2 0.0 copy-done
  255.2 0.1 convert_element_type.12
  255.3 1.2 slice_bitcast_fusion
  256.6 0.7 fusion
  257.2 0.0 copy-done.3
  257.3 1.1 maximum_convert_fusion
  258.4 0.1 slice_bitcast_fusion.7
  258.5 1.1 maximum_convert_fusion.1
  259.6 0.8 constant_dynamic-slice_fusion
  260.3 0.5 slice_bitcast_fusion.10
  260.9 4.4 %copy.48 = f32[4,320,768]{2,1,0:T(8,128)} copy(f32[4,320,768]{2,1,0:T(8,128)} %bitcast.42) | data formatting | bytes 7864320
  (25 shorter events, 0.1 us)
Async XLA Ops:
  0.7 2.1 copy-start.5
  0.7 2.1 copy-start.6
  0.7 2.1 copy-start.7
  0.7 2.1 copy-start.8
  0.7 2.2 copy-start.9
  0.7 2.2 copy-start.10
  150.4 1.5 copy-start.1
  253.6 1.5 copy-start
  255.3 1.2 copy-start.4
  255.3 1.9 copy-start.3
  257.2 1.2 copy-start.2

commit v4 on v3

--- a/solution.py
+++ b/solution.py
@@ -240,7 +240,10 @@
 QP = 112
 PIECES = 16
 SQ, SK, SV, SO, CK, CV, CQ, CO, EX, CT = 0, 1, 2, 3, 4, 5, 6, 7, 8, 12
-WINDOW = 4
+WINDOW = 2
+FIRST_DUE = 7.0
+UNIT_TIME = 3.5
+EXCHANGE_TIME = 16.0
 VMEM_BYTES = 60 * 2**20
 
 
@@ -285,20 +288,28 @@
 
 
 def weight_row(piece, owner):
-    if piece < CT:
-        return pl.multiple_of(piece * D + owner * 96, 96)
-    return pl.multiple_of(CT * D + owner * 384 + (piece - CT) * 96, 96)
+    if isinstance(piece, int) and piece >= CT:
+        return pl.multiple_of(CT * D + owner * 384 + (piece - CT) * 96, 96)
+    return pl.multiple_of(piece * D + owner * 96, 96)
+
+
+UNITS = ((SQ, SK), (SV,), (CK, CV), (SO,), (CQ,), (CO,), (8,), (9,), (10,), (11,), (12,), (13,), (14,), (15,))
+LAG = 2
 
 
 class Gather:
-    def __init__(self, shards, full, local, send, recv):
-        self.shards, self.full = shards, full
+    def __init__(self, shards, full, local, send, recv, saved, save):
+        self.shards, self.full, self.saved, self.save = shards, full, saved, save
         self.local, self.send, self.recv = local, send, recv
         self.d, self.other, self.beside, self.above, self.across = places()
         self.z = lax.axis_index("mem")
+        self.q = lax.rem(self.z, 2)
+        self.near = self.z + 1 - 2 * self.q
         self.sent = []
         self.done = 0
+        self.clock = 0.0
         self.landed = [False] * PIECES
+        self.unit_of = {piece: place for place, unit in enumerate(UNITS) for piece in unit}
 
     def at(self, piece, owner):
         return self.full.at[pl.ds(weight_row(piece, owner), 96)]
@@ -310,68 +321,135 @@
             return self.shards[EX].at[:, pl.ds((piece - EX) * D, D)]
         return self.shards[EX + 1].at[pl.ds((piece - CT) * 96, 96)]
 
-    def copy(self, src, piece, owner, kind, target):
+    def copy(self, src, piece, owner, kind, target, note):
         return pltpu.make_async_remote_copy(
             src,
             self.at(piece, owner),
-            self.send.at[piece, kind],
+            self.send.at[piece, note],
             self.recv.at[piece, kind],
-            device_id=(target, self.z),
+            device_id=target,
             device_id_type=MESH,
         )
 
     def push(self, src, piece, owner, kind, target):
-        one = self.copy(src, piece, owner, kind, target)
+        one = self.copy(src, piece, owner, kind, (target, self.z), kind)
         one.start()
         self.sent.append(one)
 
+    def lend(self, piece, owner, kind):
+        one = self.copy(self.at(piece, owner), piece, owner, kind, (self.d, self.near), 7 + kind)
+        one.start()
+        self.sent.append(one)
+
     def arrived(self, piece, kind):
-        self.copy(self.at(piece, self.d), piece, self.d, kind, self.other).wait_recv()
-
-    def start(self, piece):
-        if piece >= PIECES:
+        self.copy(self.at(piece, self.d), piece, self.d, kind, (self.other, self.z), kind).wait_recv()
+
+    def roles(self, unit):
+        first, second = unit
+        mine = first + self.q * (second - first)
+        return mine, first + second - mine
+
+    def local_copy(self, piece):
+        return pltpu.make_async_copy(self.own(piece), self.at(piece, self.d), self.local.at[piece])
+
+    def start(self, place):
+        if place >= len(UNITS):
             return
-        src = self.own(piece)
-        pltpu.make_async_copy(src, self.at(piece, self.d), self.local.at[piece]).start()
+        unit = UNITS[place]
+        if len(unit) == 1:
+            piece = unit[0]
+            src = self.own(piece)
+            self.local_copy(piece).start()
+        else:
+            piece, theirs = self.roles(unit)
+            src = self.at(piece, self.d)
+            self.push(self.at(theirs, self.d), theirs, self.d, 3, self.other)
         self.push(src, piece, self.d, 0, self.beside)
         self.push(src, piece, self.d, 1, self.above)
         self.push(src, piece, self.d, 3, self.other)
 
+    def prepare(self):
+        for unit in UNITS:
+            if len(unit) == 2:
+                for piece in unit:
+                    self.local_copy(piece).start()
+
     def begin(self):
-        for piece in range(WINDOW):
-            self.start(piece)
-
-    def finish(self, piece):
+        for unit in UNITS:
+            if len(unit) == 2:
+                for piece in unit:
+                    self.local_copy(piece).wait()
+        for place in range(WINDOW):
+            self.start(place)
+
+    def relay(self, place):
+        unit = UNITS[place]
+        piece = unit[0] if len(unit) == 1 else self.roles(unit)[0]
+        for kind, owner, side, target in ((0, self.beside, 0, self.above), (1, self.above, 1, self.beside)):
+            self.arrived(piece, kind)
+            if place % 2 == side:
+                self.push(self.at(piece, owner), piece, owner, 2, target)
+            self.push(self.at(piece, owner), piece, owner, 4 + kind, self.other)
+            if len(unit) == 2:
+                self.lend(piece, owner, kind)
+
+    def finish(self, place):
+        unit = UNITS[place]
+        piece = unit[0] if len(unit) == 1 else self.roles(unit)[0]
         self.arrived(piece, 2)
         self.push(self.at(piece, self.across), piece, self.across, 6, self.other)
+        if len(unit) == 2:
+            self.lend(piece, self.across, 2)
+
+    def borrow(self, place):
+        unit = UNITS[place]
+        if len(unit) == 2:
+            piece = self.roles(unit)[1]
+            for kind, owner in enumerate((self.beside, self.above, self.across)):
+                self.arrived(piece, kind)
+                self.push(self.at(piece, owner), piece, owner, 4 + kind, self.other)
 
     def step(self):
-        piece = self.done
-        if piece > PIECES:
+        place = self.done
+        if place >= len(UNITS) + LAG:
             return
         self.done += 1
-        if piece < PIECES:
-            self.arrived(piece, 0)
-            if piece % 2 == 0:
-                self.push(self.at(piece, self.beside), piece, self.beside, 2, self.above)
-            self.push(self.at(piece, self.beside), piece, self.beside, 4, self.other)
-            self.arrived(piece, 1)
-            if piece % 2 == 1:
-                self.push(self.at(piece, self.above), piece, self.above, 2, self.beside)
-            self.push(self.at(piece, self.above), piece, self.above, 5, self.other)
-            self.start(piece + WINDOW)
-        if piece >= 1:
-            self.finish(piece - 1)
+        if place < len(UNITS):
+            self.relay(place)
+            self.start(place + WINDOW)
+        if 1 <= place <= len(UNITS):
+            self.finish(place - 1)
+        if place >= LAG:
+            self.borrow(place - LAG)
+
+    def due(self, place):
+        return FIRST_DUE + UNIT_TIME * place
+
+    def spend(self, time):
+        self.wait_for(self.clock + time)
+
+    def wait_for(self, clock):
+        self.clock = max(self.clock, clock)
+        while self.done < len(UNITS) + LAG and self.due(self.done) <= self.clock:
+            self.step()
+
+    def upto(self, count):
+        while self.done < min(count, len(UNITS) + LAG):
+            self.clock = max(self.clock, self.due(self.done))
+            self.step()
 
     def ready(self, piece):
-        while self.done <= piece + 1:
-            self.step()
+        place = self.unit_of[piece]
+        self.upto(place + 1 + (1 if len(UNITS[place]) == 1 else LAG))
         if self.landed[piece]:
             return
         self.landed[piece] = True
-        pltpu.make_async_copy(self.own(piece), self.at(piece, self.d), self.local.at[piece]).wait()
+        if len(UNITS[place]) == 1:
+            self.local_copy(piece).wait()
         for kind in range(3, 7):
             self.arrived(piece, kind)
+        if piece < CT:
+            self.save(self.full.at[pl.ds(piece * D, D)], self.saved.at[pl.ds(piece * D, D)])
 
     def close(self):
         for one in self.sent:
@@ -393,22 +471,17 @@
 
 
 def forward_kernel(images, queries, mem_rows, *refs):
-    (tok, mem, lens, norms, *rest) = refs
+    (raw, mem, lens, *rest) = refs
+    norms, rest = rest[:6], rest[6:]
     shards = rest[:10]
     (o_result, o_full, o_acts, o_ffn, o_us, o_inv, o_kv, o_pc, o_ps, o_wst) = rest[10:20]
     (
-        full, acts, ffn, us, inv, kv, pc, ps, wst, wide, stats, osend, orecv, srecv, fst,
+        full, acts, ffn, us, inv, kv, pc, ps, wst, tok, wide, stats, osend, orecv, lsend, lrecv, fst,
         local, send, recv, zsend, zrecv, keep,
     ) = rest[20:]
     rows = images * QP
     z = lax.axis_index("mem")
     d = lax.axis_index("dp")
-    gather = Gather(shards, full, local, send, recv)
-    others = [lax.rem(z + r, 4) for r in range(1, 4)]
-    greet(
-        [(gather.other, z), (gather.beside, z), (gather.above, z)] + [(d, other) for other in others]
-    )
-    gather.begin()
     kept = []
 
     def save(src, dst):
@@ -416,8 +489,19 @@
         one.start()
         kept.append(one)
 
+    gather = Gather(shards, full, local, send, recv, o_full, save)
+    others = [lax.rem(z + r, 4) for r in range(1, 4)]
+    gather.prepare()
+    greet(
+        [(gather.other, z), (gather.beside, z), (gather.above, z)] + [(d, other) for other in others]
+    )
+    gather.begin()
+    blank = jnp.zeros((QP - queries, D), LOW)
+    for i in range(images):
+        tok[pl.ds(i * QP, QP), :] = jnp.concatenate([raw[i], blank], axis=0)
+
     def weight(piece, tile):
-        return full[pl.ds(piece * D, D), pl.ds(pl.multiple_of(tile * 256, 256), 256)]
+        return full[pl.ds(piece * D, D), cols(tile)]
 
     def cols(tile):
         return pl.ds(pl.multiple_of(tile * 256, 256), 256)
@@ -442,33 +526,28 @@
     gather.ready(SV)
     project_rows(tok, SV, 2, 1.0)
 
-    def self_image(i, carry):
+    gather.spend(2.0)
+    for i in range(images):
         at = image(i)
         valid = lax.broadcasted_iota(jnp.int32, (2 * QP, QP), 1) < queries
-        for hp in range(PAIRS):
-            lanes = pl.ds(hp * 128, 128)
+
+        def self_pair(hp, carry):
+            lanes = pl.ds(pl.multiple_of(hp * 128, 128), 128)
             scores = mm_nt(two_heads(acts[0, at, lanes]), acts[1, at, lanes])
             scores = jnp.where(valid, scores, -1e30)
             grown = jnp.exp(scores - jnp.max(scores, axis=-1, keepdims=True))
             probs = (grown / jnp.sum(grown, axis=-1, keepdims=True)).astype(LOW)
             ps[i, hp] = probs
             acts[3, at, lanes] = one_pair(mm(probs, acts[2, at, lanes])).astype(LOW)
-        return carry
-
-    lax.fori_loop(0, images, self_image, 0)
-    gather.step()
+            return carry
+
+        lax.fori_loop(0, PAIRS, self_pair, 0)
+        gather.spend(1.0)
 
     def memory_rows(piece, dst):
-        def body(i, carry):
-            at = pl.ds(pl.multiple_of(i * mem_rows, mem_rows), mem_rows)
-
-            def inner(tile, carry):
-                kv[dst, at, cols(tile)] = mm(mem[at, :], weight(piece, tile)).astype(LOW)
-                return carry
-
-            return lax.fori_loop(0, 3, inner, carry)
-
-        lax.fori_loop(0, images, body, 0)
+        for tile in range(3):
+            kv[dst, :, cols(tile)] = mm(mem[...], weight(piece, tile)).astype(LOW)
+            gather.spend(0.7)
 
     def add_branch(src, piece, base):
         def body(tile, carry):
@@ -480,7 +559,7 @@
     def normalize(which, low_dst):
         def body(i, carry):
             at = image(i)
-            gain, shift = norms[pl.ds(2 * which, 1), :], norms[pl.ds(2 * which + 1, 1), :]
+            gain, shift = norms[2 * which][...][None, :], norms[2 * which + 1][...][None, :]
             out, normed, inverse = norm_rows(wide[0, at, :], gain, shift)
             us[which, at, :] = normed
             lane = lax.broadcasted_iota(jnp.int32, (QP, 128), 1)
@@ -496,6 +575,8 @@
     gather.ready(SO)
     add_branch(3, SO, lambda at: tok[:, at].astype(WIDE))
     normalize(0, 4)
+    gather.spend(1.6)
+    save(us.at[0], o_us.at[0])
     gather.ready(CK)
     memory_rows(CK, 0)
     gather.ready(CV)
@@ -505,33 +586,6 @@
     gather.ready(CQ)
     project_rows(acts.at[4], CQ, 5, 0.125)
 
-    def cross_image(i, carry):
-        at = image(i)
-        tokens = pl.ds(pl.multiple_of(i * mem_rows, mem_rows), mem_rows)
-        place = z * mem_rows + lax.broadcasted_iota(jnp.int32, (2 * QP, mem_rows), 1)
-        valid = place < lens[i]
-        lane = lax.broadcasted_iota(jnp.int32, (QP, 128), 1)
-        noted = jnp.zeros((QP, 128), WIDE)
-        for hp in range(PAIRS):
-            lanes = pl.ds(hp * 128, 128)
-            scores = mm_nt(two_heads(acts[5, at, lanes]), kv[0, tokens, lanes])
-            scores = jnp.where(valid, scores, -1e30)
-            top = jnp.max(scores, axis=-1, keepdims=True)
-            grown = jnp.where(valid, jnp.exp(scores - top), 0.0)
-            total = jnp.sum(grown, axis=-1, keepdims=True)
-            probs = grown.astype(LOW)
-            pc[i, hp] = probs
-            osend[i, :, lanes] = one_pair(mm(probs, kv[1, tokens, lanes])).astype(LOW)
-            for half in range(2):
-                head = 2 * hp + half
-                part = pl.ds(half * QP, QP)
-                span = slice(half * QP, half * QP + QP)
-                noted = jnp.where(lane == head, top[span], noted)
-                noted = jnp.where(lane == 64 + head, total[span], noted)
-        stats[i] = noted
-        return carry
-
-    lax.fori_loop(0, images, cross_image, 0)
     pushed = []
 
     def pass_on(src, dst, kind, r):
@@ -548,45 +602,83 @@
             device_id=(d, others[r - 1]), device_id_type=MESH,
         ).wait_recv()
 
-    for r in range(1, 4):
-        pass_on(osend.at[others[r - 1]], orecv.at[r - 1], 0, r)
-        pass_on(stats.at[others[r - 1]], srecv.at[r - 1], 1, r)
+    lane = lax.broadcasted_iota(jnp.int32, (QP, 128), 1)
+
+    def turned(tall):
+        return jnp.concatenate([tall, jnp.zeros((128 - QP, 128), WIDE)], axis=0).T[:16]
+
+    def returned(flat):
+        return jnp.concatenate([flat, jnp.zeros((112, 128), WIDE)], axis=0).T[:QP]
+
+    for turn in range(4):
+        i = others[turn] if turn < 3 else z
+        at = image(i)
+        tokens = pl.ds(pl.multiple_of(i * mem_rows, mem_rows), mem_rows)
+        place = z * mem_rows + lax.broadcasted_iota(jnp.int32, (2 * QP, mem_rows), 1)
+        valid = place < lens[i]
+
+        def pair(hp, noted):
+            lanes = pl.ds(pl.multiple_of(hp * 128, 128), 128)
+            scores = mm_nt(two_heads(acts[5, at, lanes]), kv[0, tokens, lanes])
+            scores = jnp.where(valid, scores, -1e30)
+            top = jnp.max(scores, axis=-1, keepdims=True)
+            grown = jnp.where(valid, jnp.exp(scores - top), 0.0)
+            total = jnp.sum(grown, axis=-1, keepdims=True)
+            shrink = jnp.where(total > 0.0, 1.0 / total, 0.0)
+            probs = grown.astype(LOW)
+            pc[i, hp] = probs
+            osend[turn, :, lanes] = one_pair(mm(probs, kv[1, tokens, lanes]) * shrink).astype(LOW)
+            for half in range(2):
+                span = slice(half * QP, half * QP + QP)
+                noted = jnp.where(lane == 2 * hp + half, top[span], noted)
+                noted = jnp.where(lane == 64 + 2 * hp + half, total[span], noted)
+            return noted
+
+        noted = lax.fori_loop(0, PAIRS, pair, jnp.zeros((QP, 128), WIDE))
+        stats[i] = noted
+        total = pltpu.roll(noted, 64, 1)
+        lsend[turn] = turned(jnp.where(total > 0.0, noted + jnp.log(total), -1e30))
+        if turn < 3:
+            pass_on(osend.at[turn], orecv.at[turn], 0, turn + 1)
+            pass_on(lsend.at[turn], lrecv.at[turn], 1, turn + 1)
+        gather.spend(1.9)
     save(pc, o_pc)
-    gather.ready(CO)
+    gather.wait_for(gather.clock + EXCHANGE_TIME - 5.0)
     for r in range(1, 4):
         taken(orecv.at[r - 1], 0, r)
-        taken(srecv.at[r - 1], 1, r)
-    noted = [stats[z], srecv[0], srecv[1], srecv[2]]
+        taken(lrecv.at[r - 1], 1, r)
+    noted = [lsend[3], lrecv[0], lrecv[1], lrecv[2]]
     top = functools.reduce(jnp.maximum, noted)
-    scale = [jnp.exp(one - top) for one in noted]
-    total = sum(s * pltpu.roll(one, 64, 1) for s, one in zip(scale, noted))
-    shrink = 1.0 / total
-    lane = lax.broadcasted_iota(jnp.int32, (QP, 128), 1)
-    fst[z] = jnp.where(lane < 64, top, pltpu.roll(shrink, 64, 1))
+    level = top + jnp.log(sum(jnp.exp(one - top) for one in noted))
+    fst[z] = level
+    share = [returned(jnp.exp(one - level)) for one in noted]
     lower = low_lanes((QP, 128))
     mine = image(z)
     for hp in range(PAIRS):
         lanes = pl.ds(hp * 128, 128)
         joined = jnp.zeros((QP, 128), WIDE)
         for r in range(4):
-            share = scale[r] * shrink
-            spread = jnp.where(lower, share[:, 2 * hp : 2 * hp + 1], share[:, 2 * hp + 1 : 2 * hp + 2])
-            part = osend[z, :, lanes] if r == 0 else orecv[r - 1, :, lanes]
+            spread = jnp.where(
+                lower, share[r][:, 2 * hp : 2 * hp + 1], share[r][:, 2 * hp + 1 : 2 * hp + 2]
+            )
+            part = osend[3, :, lanes] if r == 0 else orecv[r - 1, :, lanes]
             joined = joined + spread * part.astype(WIDE)
         acts[6, mine, lanes] = joined.astype(LOW)
     for r in range(1, 4):
         pass_on(acts.at[6, mine], acts.at[6, mine], 2, r)
         pass_on(fst.at[z], fst.at[z], 3, r)
+    gather.wait_for(gather.clock + EXCHANGE_TIME)
+    gather.ready(CO)
     for r in range(1, 4):
         back = lax.rem(z + 4 - r, 4)
         taken(acts.at[6, image(back)], 2, r)
         taken(fst.at[back], 3, r)
     for i in range(images):
-        final = fst[i]
-        wst[i] = jnp.exp(stats[i] - final) * pltpu.roll(final, 64, 1)
+        wst[i] = jnp.exp(stats[i] - returned(fst[i]))
     save(wst, o_wst)
     add_branch(6, CO, lambda at: wide[1, :, at])
     normalize(1, 7)
+    save(us.at[1], o_us.at[1])
     save(acts, o_acts)
 
     def expand(block):
@@ -607,10 +699,11 @@
     for block in range(4):
         gather.ready(EX + block)
         expand(block)
+        gather.spend(1.2)
     save(ffn, o_ffn)
     for block in range(4):
         gather.ready(CT + block)
-    save(full, o_full)
+    save(full.at[pl.ds(CT * D, FF)], o_full.at[pl.ds(CT * D, FF)])
 
     def contract(tile, carry):
         wide[0, :, cols(tile)] = wide[1, :, cols(tile)] + mm(
@@ -621,7 +714,7 @@
     lax.fori_loop(0, 3, contract, 0)
     normalize(2, None)
     save(wide.at[1], o_result)
-    save(us, o_us)
+    save(us.at[2], o_us.at[2])
     save(inv, o_inv)
     for one in pushed:
         one.wait_send()
@@ -650,28 +743,30 @@
     return pl.pallas_call(
         functools.partial(forward_kernel, images, queries, mem_rows),
         out_shape=outs,
-        in_specs=[INNER, INNER, SCALAR, INNER] + [ANY] * 10,
+        in_specs=[INNER, INNER, SCALAR] + [INNER] * 6 + [ANY] * 10,
         out_specs=[ANY] * len(outs),
         scratch_shapes=[
             *[pltpu.VMEM(one.shape, one.dtype) for one in outs[1:]],
+            pltpu.VMEM((rows, D), LOW),
             pltpu.VMEM((2, rows, D), WIDE),
             pltpu.VMEM((images, QP, 128), WIDE),
-            pltpu.VMEM((images, QP, D), LOW),
+            pltpu.VMEM((4, QP, D), LOW),
             pltpu.VMEM((3, QP, D), LOW),
-            pltpu.VMEM((3, QP, 128), WIDE),
-            pltpu.VMEM((images, QP, 128), WIDE),
+            pltpu.VMEM((4, 16, 128), WIDE),
+            pltpu.VMEM((3, 16, 128), WIDE),
+            pltpu.VMEM((images, 16, 128), WIDE),
             dma((PIECES,)),
-            dma((PIECES, 7)),
+            dma((PIECES, 10)),
             dma((PIECES, 7)),
             dma((4, 3)),
             dma((4, 3)),
-            dma((12,)),
+            dma((28,)),
         ],
         compiler_params=pltpu.CompilerParams(
             collective_id=0, has_side_effects=True, vmem_limit_bytes=VMEM_BYTES
         ),
         name="forward",
-    )(tok, mem, lens, norms, *(shards[place] for place in (0, 1, 2, 3, 5, 6, 4, 7, 8, 9)))
+    )(tok, mem, lens, *norms, *(shards[place] for place in (0, 1, 2, 3, 5, 6, 4, 7, 8, 9)))
 
 
 def rows_of_image(i):
@@ -732,16 +827,16 @@
 
 def backward_kernel(images, queries, mem_rows, *refs):
     (
-        h_norms, h_cot, h_tok, h_mem, h_full, h_acts, h_ffn, h_us, h_inv, h_kv, h_pc, h_ps, h_wst,
-    ) = refs[:13]
-    (o_expand, o_contract, o_rest, o_keys, o_mem, o_in, o_norms) = refs[13:20]
+        h_gain_one, h_gain_two, h_gain_three, h_cot, h_tok, h_mem, h_full, h_acts, h_ffn, h_us, h_inv, h_kv, h_pc, h_ps, h_wst,
+    ) = refs[:15]
+    (o_expand, o_contract, o_rest, o_keys, o_mem, o_in, o_norms) = refs[15:22]
     (
-        norms, cot, tok, mem, slots, acts, ffn, us, inv, kv, pc, ps, wst, wide, grads, nsum, nin,
+        cot, tok, mem, slots, acts, ffn, us, inv, kv, pc, ps, wst, wide, grads, nsum, nin,
         zsend, zin, mout,
         g_expand, g_contract, g_rest, c_expand, c_contract, c_rest, c_keys,
         t_expand, t_contract, t_rest, t_keys, f_expand, f_contract, f_rest, k_out, k_in,
         load, slot_sems, pc_sems, mout_sems, core_sems, chip_sems, fin_sems, local_sems, ksems, zsems, nsems,
-    ) = refs[20:]
+    ) = refs[22:]
     z = lax.axis_index("mem")
     d = lax.axis_index("dp")
     where = places()
@@ -750,6 +845,7 @@
     others = [lax.rem(z + r, 4) for r in range(1, 4)]
     dpeers = [lax.rem(d + r, 8) for r in range(1, 8)]
 
+    gains = (h_gain_one, h_gain_two, h_gain_three)
     loads = {}
     waited = set()
 
@@ -770,7 +866,6 @@
         if turn < len(order):
             slot_copy(turn).start()
 
-    fetch("norms", h_norms, norms)
     fetch("cot", h_cot, cot)
     fetch("inv", h_inv, inv)
     fetch("u3", h_us.at[2], us.at[0])
@@ -807,7 +902,7 @@
             above = incoming(at)
             unit = us[slot, at, :]
             inverse = inv[at, which : which + 1]
-            scaled = above * norms[2 * which : 2 * which + 1, :]
+            scaled = above * gains[which][...][None, :]
             first = jnp.mean(scaled, axis=-1, keepdims=True)
             second = jnp.mean(scaled * unit, axis=-1, keepdims=True)
             grad = inverse * (scaled - first - unit * second)
@@ -830,7 +925,7 @@
     def freed(piece):
         prefetch(turn_of[piece] + depth)
 
-    for name in ("norms", "cot", "inv", "u3"):
+    for name in ("cot", "inv", "u3"):
         have(name)
     norm_back(2, lambda at: cot[at, :].astype(WIDE), 0, 0)
     fetch("u1", h_us.at[0], us.at[0])
@@ -994,9 +1089,9 @@
 
         def body(tile, carry):
             span = cols_of_tile(tile)
-            mout[i % 2, :, span] = mm_nt(kv[0, at, :], key_weight[span, :]) + mm_nt(
-                kv[1, at, :], value_weight[span, :]
-            )
+            mout[i % 2, :, span] = (
+                mm_nt(kv[0, at, :], key_weight[span, :]) + mm_nt(kv[1, at, :], value_weight[span, :])
+            ).astype(LOW)
             return carry
 
         lax.fori_loop(0, 3, body, 0)
@@ -1156,7 +1251,7 @@
         reducer.settle()
 
 
-def backward(norms, cot, tok, mem, saved, images, queries, mem_rows):
+def backward(gains, cot, tok, mem, saved, images, queries, mem_rows):
     full, acts, ffn, us, inv, kv, pc, ps, wst = saved
     rows = images * QP
     tokens = images * mem_rows
@@ -1166,7 +1261,7 @@
         shape((2, 384, 384), LOW),
         shape((3, 2, 96, D), LOW),
         shape((24, 1536), WIDE),
-        shape((tokens, D), WIDE),
+        shape((tokens, D), LOW),
         shape((rows, D), WIDE),
         shape((8, D), WIDE),
     )
@@ -1175,10 +1270,9 @@
     return pl.pallas_call(
         functools.partial(backward_kernel, images, queries, mem_rows),
         out_shape=outs,
-        in_specs=[ANY] * 13,
+        in_specs=[INNER] * 3 + [ANY] * 12,
         out_specs=[ANY] * 3 + [INNER] + [ANY] * 2 + [INNER],
         scratch_shapes=[
-            vmem((8, D), WIDE),
             vmem((rows, D), LOW),
             vmem((rows, D), LOW),
             vmem((tokens, D), LOW),
@@ -1197,7 +1291,7 @@
             vmem((7, 8, D), WIDE),
             vmem((4, QP, D), LOW),
             vmem((3, QP, D), LOW),
-            vmem((2, mem_rows, D), WIDE),
+            vmem((2, mem_rows, D), LOW),
             vmem((2, 4, 96, 1536), LOW),
             vmem((2, 4, 384, 384), LOW),
             vmem((3, 2, 4, 96, D), LOW),
@@ -1230,7 +1324,7 @@
             collective_id=1, has_side_effects=True, vmem_limit_bytes=VMEM_BYTES
         ),
         name="backward",
-    )(norms, cot, tok, mem, *saved)
+    )(*gains, cot, tok, mem, *saved)
 
 
 def fused_on_device(
@@ -1257,7 +1351,7 @@
 ):
     images, queries, width = inputs.shape
     mem_rows = memory.shape[1]
-    norms = jnp.stack([gain_one, shift_one, gain_two, shift_two, gain_three, shift_three, gain_one, gain_one])
+    norms = (gain_one, shift_one, gain_two, shift_two, gain_three, shift_three)
     shards = (self_query, self_key, self_value, self_out, cross_query, cross_key, cross_value, cross_out, expand_weight, contract_weight)
 
     def padded(values):
@@ -1270,10 +1364,10 @@
     tokens = padded(inputs)
     memory_flat = memory.reshape(images * mem_rows, width)
     result, full, acts, ffn, us, inv, kv, pc, ps, wst = forward(
-        tokens, memory_flat, lengths, norms, shards, images, queries, mem_rows
+        inputs, memory_flat, lengths, norms, shards, images, queries, mem_rows
     )
     spread, contracted, rest, keys, memory_grad, input_grad, sums = backward(
-        norms, padded(cotangent), tokens, memory_flat, (full, acts, ffn, us, inv, kv, pc, ps, wst),
+        norms[::2], padded(cotangent), tokens, memory_flat, (full, acts, ffn, us, inv, kv, pc, ps, wst),
         images, queries, mem_rows,
     )
     share = self_query.shape[0]
@@ -1282,7 +1376,7 @@
     return (
         cut(result),
         cut(input_grad),
-        memory_grad.reshape(memory.shape),
+        memory_grad.reshape(memory.shape).astype(WIDE),
         rest[1, 1],
         rest[2, 0],
         rest[2, 1],

time: 268 us -> 223 us (0.83)
  Pallas kernels: 245 us -> 204 us
  local copies, waits for them, and re-layouts: 17.2 us -> 13.4 us
    pallas_call x1, Pallas kernels: 145 us -> 106 us  [forward(): pl.pallas_call(functools.partial(forward_kernel, images, queries, mem_row...]
    unnamed x27 -> x18, local copies, waits for them, and re-layouts: 8.7 us -> 5.57 us
where the time goes in v4:
time: 223 us
  Pallas kernels  204 us (91%)
  local copies, waits for them, and re-layouts  13.4 us (6%)
  other arithmetic  4.61 us (2%)
    pallas_call x1, Pallas kernels, forward(): pl.pallas_call(functools.partial(forward_kernel, images, queries, mem_row...  106 us
    pallas_call x1, Pallas kernels, backward(): pl.pallas_call(functools.partial(backward_kernel, images, queries, mem_ro...  98 us
    unnamed x18, local copies, waits for them, and re-layouts  5.57 us

profile of v4, /device:TPU:0, one launch (start us, length us, event | category | flops | bytes accessed | tf_op | source)
XLA Modules:
  0.0 222.8 jit_solution(17121301974060936105)
XLA Ops:
  0.7 2.0 copy.39.refs_0_
  2.6 106.1 %forward.1 = (f32[448,768]{1,0:T(8,128)}, bf16[12288,768]{1,0:T(8,128)(2,1)}, bf16[8,448,768]{2,1,0:T(8,128)(2,1)}, bf16[2,448,3072]{2,1,0:T(8,128)(2,1)}, f32[3...) custom-call(bf16[4,100,768]{2,1,0:T(8,128)(2,1)} %copy.39.refs_0_, ...), custom_call_target="tpu_custom_call" | custom-call | tf_op jit(solution)/shard_map/forward/pallas_call | solution.py:743
  108.7 1.4 slice.80
  110.1 0.0 copy-start.3
  110.1 1.5 copy.44
  111.6 0.0 copy-done.3
  111.6 0.1 copy.46
  111.7 0.9 pad.7.clone
  112.6 0.3 copy-done
  112.8 0.9 pad.8.clone
  113.7 98.0 %backward.1 = (bf16[2,96,1536]{2,1,0:T(8,128)(2,1)}, bf16[2,384,384]{2,1,0:T(8,128)(2,1)}, bf16[3,2,96,768]{3,2,1,0:T(8,128)(2,1)}, f32[24,1536]{1,0:T(8,128)}, ...) custom-call(f32[768]{0:T(1024)} %refs_0_.2, f32[768]{0:T(1024)} %refs_1_.1, f32[768]{0:T(1024)} %refs_2_.3, ...), custom_call_target="tpu_custom_call" | custom-call | tf_op jit(solution)/shard_map/backward/pallas_call | solution.py:1270
  211.7 1.4 slice.81
  213.1 1.5 copy.45
  214.6 0.2 copy-done.1
  214.9 2.3 %convert.1 = f32[4,320,768]{2,1,0:T(8,128)} convert(bf16[4,320,768]{2,1,0:T(8,128)(2,1)S(1)} %bitcast.43) | non-fusion elementwise | flops 983040 | bytes 5898240 | tf_op jit(solution)/shard_map/convert_element_type | solution.py:1379
  217.1 0.1 convert_element_type.20
  217.3 1.2 slice_bitcast_fusion
  218.5 0.7 fusion
  219.2 1.1 maximum_convert_fusion
  220.4 0.0 copy-done.4
  220.4 0.1 slice_bitcast_fusion.7
  220.4 1.1 maximum_convert_fusion.1
  221.5 0.8 constant_dynamic-slice_fusion
  222.3 0.5 slice_bitcast_fusion.10
  (10 shorter events, 0.1 us)
Async XLA Ops:
  110.1 1.5 copy-start.3
  111.6 1.2 copy-start
  213.1 1.8 copy-start.1
  214.9 2.3 %copy-start.2 = (bf16[3,2,96,768]{3,2,1,0:T(8,128)(2,1)S(1)}, bf16[3,2,96,768]{3,2,1,0:T(8,128)(2,1)}, u32[]{:S(2)}) copy-start(bf16[3,2,96,768]{3,2,1,0:T(8,128)(2,1)} %get-tuple-element.48) | copy-start | bytes 2654212
  217.3 1.2 copy-start.6
  217.3 1.9 copy-start.5
  219.2 1.2 copy-start.4

commit v5 on v4

--- a/solution.py
+++ b/solution.py
@@ -306,6 +306,7 @@
         self.q = lax.rem(self.z, 2)
         self.near = self.z + 1 - 2 * self.q
         self.sent = []
+        self.role = {}
         self.done = 0
         self.clock = 0.0
         self.landed = [False] * PIECES
@@ -345,9 +346,11 @@
         self.copy(self.at(piece, self.d), piece, self.d, kind, (self.other, self.z), kind).wait_recv()
 
     def roles(self, unit):
-        first, second = unit
-        mine = first + self.q * (second - first)
-        return mine, first + second - mine
+        if unit not in self.role:
+            first, second = unit
+            mine = first + self.q * (second - first)
+            self.role[unit] = (mine, first + second - mine)
+        return self.role[unit]
 
     def local_copy(self, piece):
         return pltpu.make_async_copy(self.own(piece), self.at(piece, self.d), self.local.at[piece])
@@ -829,14 +832,15 @@
     (
         h_gain_one, h_gain_two, h_gain_three, h_cot, h_tok, h_mem, h_full, h_acts, h_ffn, h_us, h_inv, h_kv, h_pc, h_ps, h_wst,
     ) = refs[:15]
-    (o_expand, o_contract, o_rest, o_keys, o_mem, o_in, o_norms) = refs[15:22]
+    (o_expand, o_contract, o_co, o_mid, o_late, o_last, o_keys, o_mem, o_in, o_norms) = refs[15:25]
     (
         cot, tok, mem, slots, acts, ffn, us, inv, kv, pc, ps, wst, wide, grads, nsum, nin,
         zsend, zin, mout,
-        g_expand, g_contract, g_rest, c_expand, c_contract, c_rest, c_keys,
-        t_expand, t_contract, t_rest, t_keys, f_expand, f_contract, f_rest, k_out, k_in,
+        g_expand, g_contract, g_co, g_mid, g_late, g_last, c_expand, c_contract, c_co, c_mid, c_late, c_last, c_keys,
+        t_expand, t_contract, t_co, t_mid, t_late, t_last, t_keys,
+        f_expand, f_contract, f_co, f_mid, f_late, f_last, k_out, k_in,
         load, slot_sems, pc_sems, mout_sems, core_sems, chip_sems, fin_sems, local_sems, ksems, zsems, nsems,
-    ) = refs[22:]
+    ) = refs[25:]
     z = lax.axis_index("mem")
     d = lax.axis_index("dp")
     where = places()
@@ -867,19 +871,10 @@
             slot_copy(turn).start()
 
     fetch("cot", h_cot, cot)
+    fetch("u3", h_us.at[2], us.at[0])
     fetch("inv", h_inv, inv)
-    fetch("u3", h_us.at[2], us.at[0])
-    for turn in range(depth):
-        prefetch(turn)
+    prefetch(0)
     fetch("gp", h_ffn.at[1], ffn.at[1])
-    fetch("act", h_ffn.at[0], ffn.at[0])
-    fetch("acts", h_acts, acts)
-    fetch("u2", h_us.at[1], us.at[1])
-    fetch("kv", h_kv, kv)
-    fetch("wst", h_wst, wst)
-    fetch("ps", h_ps, ps)
-    fetch("mem", h_mem, mem)
-    fetch("tok", h_tok, tok)
 
     def have(name):
         if name not in waited:
@@ -890,8 +885,6 @@
         i = lax.rem(z + turn + 1, 4)
         return pltpu.make_async_copy(h_pc.at[i], pc.at[turn % 2], pc_sems.at[turn % 2])
 
-    pc_copy(0).start()
-    pc_copy(1).start()
     greet([(peer, z) for peer in dpeers] + [(d, other) for other in others])
 
     nsum[...] = jnp.zeros_like(nsum)
@@ -928,7 +921,9 @@
     for name in ("cot", "inv", "u3"):
         have(name)
     norm_back(2, lambda at: cot[at, :].astype(WIDE), 0, 0)
-    fetch("u1", h_us.at[0], us.at[0])
+    for turn in range(1, depth):
+        prefetch(turn)
+    fetch("second_low", h_acts.at[7], acts.at[7])
     have("gp")
     for block in range(4):
         weight = slot(CT + block)
@@ -945,7 +940,13 @@
     def reduce_at(place, grad, core_in, chip_in):
         return Reduce(where, place, grad, core_in, chip_in, core_sems, chip_sems)
 
-    have("acts")
+    fetch("u2", h_us.at[1], us.at[1])
+    fetch("kv", h_kv, kv)
+    fetch("wst", h_wst, wst)
+    fetch("acts", h_acts.at[pl.ds(0, 7)], acts.at[pl.ds(0, 7)])
+    pc_copy(0).start()
+    pc_copy(1).start()
+    have("second_low")
     r_expand = reduce_at(0, g_expand, c_expand, t_expand)
 
     def expand_part(tile, carry):
@@ -957,18 +958,6 @@
 
     lax.fori_loop(0, 6, expand_part, 0)
     r_expand.core_stage()
-    have("act")
-    r_contract = reduce_at(1, g_contract, c_contract, t_contract)
-
-    def contract_part(e, carry):
-        at = pl.ds(pl.multiple_of(e * 384, 384), 384)
-        half = pl.ds(pl.multiple_of(q * 384, 384), 384)
-        g_contract[lax.rem(e, 2), e // 2] = mm_tn(ffn[0, :, at], grads[0, :, half]).astype(LOW)
-        return carry
-
-    lax.fori_loop(0, 8, contract_part, 0)
-    r_contract.core_stage()
-    r_expand.chip_stage()
     for block in range(4):
         weight = slot(EX + block)
 
@@ -980,7 +969,8 @@
 
         lax.fori_loop(0, 3, body, 0)
         freed(EX + block)
-    r_contract.chip_stage()
+        if block == 2:
+            r_expand.chip_stage()
     have("u2")
     norm_back(1, lambda at: wide[0, at, :], 1, 1)
 
@@ -994,9 +984,15 @@
         lax.fori_loop(0, 3, body, 0)
         freed(piece)
 
-    through(1, CO, 0)
+    fetch("act", h_ffn.at[0], ffn.at[0])
+    fetch("mem", h_mem, mem)
+    fetch("u1", h_us.at[0], us.at[0])
+    fetch("ps", h_ps, ps)
+    fetch("tok", h_tok, tok)
+    through(1, CO, 2)
     have("kv")
     have("wst")
+    have("acts")
     pushed = []
 
     def across_mem(src, dst, kind, r):
@@ -1015,7 +1011,7 @@
         def pair(hp, carry):
             lanes = pl.ds(pl.multiple_of(hp * 128, 128), 128)
             query = two_heads(acts[5, at, lanes])
-            above = two_heads(grads[0, at, lanes])
+            above = two_heads(grads[2, at, lanes])
             attn = acts[6, at, lanes].astype(WIDE)
             row = jnp.sum(above.astype(WIDE) * jnp.concatenate([attn, attn], axis=0), axis=-1, keepdims=True)
             lane = lax.broadcasted_iota(jnp.int32, (QP, 128), 1)
@@ -1042,12 +1038,27 @@
             one = across_mem(zsend.at[turn], zin.at[turn], 0, turn + 1)
             one.start()
             pushed.append(one)
+        if turn == 1:
+            have("act")
+            r_contract = reduce_at(1, g_contract, c_contract, t_contract)
+
+            def contract_part(e, carry):
+                at = pl.ds(pl.multiple_of(e * 384, 384), 384)
+                half = pl.ds(pl.multiple_of(q * 384, 384), 384)
+                g_contract[lax.rem(e, 2), e // 2] = mm_tn(ffn[0, :, at], grads[0, :, half]).astype(LOW)
+                return carry
+
+            lax.fori_loop(0, 8, contract_part, 0)
+            r_contract.core_stage()
+        if turn == 3:
+            r_contract.chip_stage()
 
     have("mem")
+    f_expand[...] = r_expand.total().astype(LOW)
     r_expand.settle()
     r_keys = reduce_at(2, g_expand, c_keys, t_keys)
-    for which in range(2):
-
+
+    def key_parts(which):
         def key_part(tile, carry):
             out = mm_tn(mem[...], kv[which, :, cols_of_tile(tile)]).astype(LOW)
             at = pl.ds(pl.multiple_of(which * D + tile * 256, 256), 256)
@@ -1055,11 +1066,9 @@
                 g_expand[e % 2, e // 2, :, at] = out[96 * e : 96 * e + 96]
             return carry
 
-        if which == 0:
-            final_expand = r_expand.total()
-            f_expand[...] = final_expand.astype(LOW)
         lax.fori_loop(0, 3, key_part, 0)
-    r_keys.core_stage()
+
+    key_parts(0)
     for r in range(1, 4):
         across_mem(zin.at[r - 1], zin.at[r - 1], 0, r).wait_recv()
     mine = rows_of_image(z)
@@ -1070,6 +1079,8 @@
         one = across_mem(grads.at[3, mine], grads.at[3, mine], 1, r)
         one.start()
         pushed.append(one)
+    key_parts(1)
+    r_keys.core_stage()
 
     def finals(fin, out, place):
         pltpu.make_async_copy(fin, out, local_sems.at[place]).start()
@@ -1080,7 +1091,6 @@
         return one
 
     ended = []
-    r_keys.chip_stage()
     key_weight, value_weight = slot(CK), slot(CV)
     for i in range(images):
         at = pl.ds(i * mem_rows, mem_rows)
@@ -1096,14 +1106,33 @@
 
         lax.fori_loop(0, 3, body, 0)
         pltpu.make_async_copy(mout.at[i % 2], o_mem.at[at], mout_sems.at[i % 2]).start()
+        if i == 1:
+            r_keys.chip_stage()
     freed(CK)
     freed(CV)
+    def wide_parts(place, grad, core_in, chip_in, left, right, tiles):
+        def body(tile, carry):
+            out = mm_tn(left(), right(cols_of_tile(tile))).astype(LOW)
+            for e in range(8):
+                grad[e % 2, e // 2, :, cols_of_tile(tile)] = out[96 * e : 96 * e + 96]
+            return carry
+
+        lax.fori_loop(0, tiles, body, 0)
+
+    def half_parts(grad, left, right):
+        half = pl.ds(pl.multiple_of(q * 384, 384), 384)
+        out = mm_tn(left, right(half)).astype(LOW)
+        for e in range(8):
+            grad[e % 2, e // 2] = out[96 * e : 96 * e + 96]
+
+    r_co = reduce_at(3, g_co, c_co, t_co)
+    half_parts(g_co, acts[6], lambda at: grads[1, :, at])
+    r_co.core_stage()
     for r in range(1, 4):
         back = lax.rem(z + 4 - r, 4)
         across_mem(grads.at[3, rows_of_image(back)], grads.at[3, rows_of_image(back)], 1, r).wait_recv()
+    r_co.chip_stage()
     ended.append(finals(f_expand, o_expand.at[q], 0))
-    f_contract[...] = r_contract.total().astype(LOW)
-    ended.append(finals(f_contract, o_contract.at[q], 1))
 
     def add_back(src, piece):
         weight = slot(piece)
@@ -1128,37 +1157,27 @@
         pushed.append(one)
     have("tok")
 
-    def rest_part(turn, lefts, rights):
-        reducer = reduce_at(3 + turn, g_rest.at[turn], c_rest.at[turn], t_rest.at[turn])
-
-        def work(left, right):
-            def body(tile, carry):
-                out = mm_tn(left(), right(cols_of_tile(tile))).astype(LOW)
-                for e in range(8):
-                    g_rest[turn, e % 2, e // 2, :, cols_of_tile(tile)] = out[96 * e : 96 * e + 96]
-                return carry
-
-            lax.fori_loop(0, 3, body, 0)
-
-        @pl.when(q == 0)
-        def _():
-            work(lefts[0], rights[0])
-
-        @pl.when(q == 1)
-        def _():
-            work(lefts[1], rights[1])
+    def either(place, grad, core_in, chip_in, lefts, rights):
+        reducer = reduce_at(place, grad, core_in, chip_in)
+        for parity in range(2):
+
+            @pl.when(q == parity)
+            def _():
+                wide_parts(place, grad, core_in, chip_in, lefts[parity], rights[parity], 3)
 
         reducer.core_stage()
         return reducer
 
-    r_first = rest_part(
-        0,
-        (lambda: acts[6], lambda: acts[4]),
-        (lambda at: grads[1, :, at], lambda at: grads[3, :, at]),
+    r_mid = either(
+        4, g_mid, c_mid, t_mid,
+        (lambda: acts[4], lambda: acts[3]),
+        (lambda at: grads[3, :, at], lambda at: grads[2, :, at]),
     )
     through(2, SO, 0)
     have("ps")
-    r_first.chip_stage()
+    r_mid.chip_stage()
+    f_contract[...] = r_contract.total().astype(LOW)
+    ended.append(finals(f_contract, o_contract.at[q], 1))
 
     def self_image(i, carry):
         at = rows_of_image(i)
@@ -1178,18 +1197,16 @@
         return carry
 
     lax.fori_loop(0, images, self_image, 0)
-    r_second = rest_part(
-        1,
-        (lambda: acts[3], lambda: tok[...]),
-        (lambda at: grads[2, :, at], lambda at: acts[0, :, at]),
-    )
-    r_third = rest_part(
-        2,
+    r_late = either(
+        5, g_late, c_late, t_late,
         (lambda: tok[...], lambda: tok[...]),
-        (lambda at: acts[1, :, at], lambda at: acts[2, :, at]),
-    )
-    r_second.chip_stage()
-    r_third.chip_stage()
+        (lambda at: acts[0, :, at], lambda at: acts[2, :, at]),
+    )
+    r_last = reduce_at(6, g_last, c_last, t_last)
+    half_parts(g_last, tok[...], lambda at: acts[1, :, at])
+    r_last.core_stage()
+    r_late.chip_stage()
+    r_last.chip_stage()
     quarter = 24
     keys_total = r_keys.total()
     for part in range(4):
@@ -1201,16 +1218,18 @@
         )
         one.start()
         pushed.append(one)
-    f_rest[0] = r_first.total().astype(LOW)
-    ended.append(finals(f_rest.at[0], o_rest.at[0, q], 2))
+    f_co[...] = r_co.total().astype(LOW)
+    ended.append(finals(f_co, o_co.at[q], 2))
+    f_mid[...] = r_mid.total().astype(LOW)
+    ended.append(finals(f_mid, o_mid.at[q], 3))
     add_back(lambda: acts[0], SQ)
     add_back(lambda: acts[1], SK)
     add_back(lambda: acts[2], SV)
     pltpu.make_async_copy(wide.at[0], o_in, load.at[15]).start()
-    f_rest[1] = r_second.total().astype(LOW)
-    ended.append(finals(f_rest.at[1], o_rest.at[1, q], 3))
-    f_rest[2] = r_third.total().astype(LOW)
-    ended.append(finals(f_rest.at[2], o_rest.at[2, q], 4))
+    f_late[...] = r_late.total().astype(LOW)
+    ended.append(finals(f_late, o_late.at[q], 4))
+    f_last[...] = r_last.total().astype(LOW)
+    ended.append(finals(f_last, o_last.at[q], 5))
     sums = nsum[...]
     for r in range(1, 8):
         pltpu.make_async_remote_copy(
@@ -1231,14 +1250,8 @@
         at = pl.ds(i * mem_rows, mem_rows)
         pltpu.make_async_copy(mout.at[i % 2], o_mem.at[at], mout_sems.at[i % 2]).wait()
     pltpu.make_async_copy(wide.at[0], o_in, load.at[15]).wait()
-    fins = (f_expand, f_contract, f_rest.at[0], f_rest.at[1], f_rest.at[2])
-    outs = (
-        (o_expand.at[q], o_expand.at[1 - q]),
-        (o_contract.at[q], o_contract.at[1 - q]),
-        (o_rest.at[0, q], o_rest.at[0, 1 - q]),
-        (o_rest.at[1, q], o_rest.at[1, 1 - q]),
-        (o_rest.at[2, q], o_rest.at[2, 1 - q]),
-    )
+    fins = (f_expand, f_contract, f_co, f_mid, f_late, f_last)
+    outs = [(out.at[q], out.at[1 - q]) for out in (o_expand, o_contract, o_co, o_mid, o_late, o_last)]
     for place, (fin, (out, theirs)) in enumerate(zip(fins, outs)):
         pltpu.make_async_copy(fin, out, local_sems.at[place]).wait()
         ended[place].wait_send()
@@ -1247,7 +1260,7 @@
         ).wait_recv()
     for one in pushed:
         one.wait_send()
-    for reducer in (r_contract, r_keys, r_first, r_second, r_third):
+    for reducer in (r_contract, r_keys, r_co, r_mid, r_late, r_last):
         reducer.settle()
 
 
@@ -1259,7 +1272,10 @@
     outs = (
         shape((2, 96, 1536), LOW),
         shape((2, 384, 384), LOW),
-        shape((3, 2, 96, D), LOW),
+        shape((2, 96, 384), LOW),
+        shape((2, 96, D), LOW),
+        shape((2, 96, D), LOW),
+        shape((2, 96, 384), LOW),
         shape((24, 1536), WIDE),
         shape((tokens, D), LOW),
         shape((rows, D), WIDE),
@@ -1271,7 +1287,7 @@
         functools.partial(backward_kernel, images, queries, mem_rows),
         out_shape=outs,
         in_specs=[INNER] * 3 + [ANY] * 12,
-        out_specs=[ANY] * 3 + [INNER] + [ANY] * 2 + [INNER],
+        out_specs=[ANY] * 6 + [INNER] + [ANY] * 2 + [INNER],
         scratch_shapes=[
             vmem((rows, D), LOW),
             vmem((rows, D), LOW),
@@ -1294,28 +1310,40 @@
             vmem((2, mem_rows, D), LOW),
             vmem((2, 4, 96, 1536), LOW),
             vmem((2, 4, 384, 384), LOW),
-            vmem((3, 2, 4, 96, D), LOW),
+            vmem((2, 4, 96, 384), LOW),
+            vmem((2, 4, 96, D), LOW),
+            vmem((2, 4, 96, D), LOW),
+            vmem((2, 4, 96, 384), LOW),
             vmem((4, 96, 1536), LOW),
             vmem((4, 384, 384), LOW),
-            vmem((3, 4, 96, D), LOW),
+            vmem((4, 96, 384), LOW),
+            vmem((4, 96, D), LOW),
+            vmem((4, 96, D), LOW),
+            vmem((4, 96, 384), LOW),
             vmem((4, 96, 1536), LOW),
             vmem((3, 96, 1536), LOW),
             vmem((3, 384, 384), LOW),
-            vmem((3, 3, 96, D), LOW),
+            vmem((3, 96, 384), LOW),
+            vmem((3, 96, D), LOW),
+            vmem((3, 96, D), LOW),
+            vmem((3, 96, 384), LOW),
             vmem((3, 96, 1536), LOW),
             vmem((96, 1536), LOW),
             vmem((384, 384), LOW),
-            vmem((3, 96, D), LOW),
+            vmem((96, 384), LOW),
+            vmem((96, D), LOW),
+            vmem((96, D), LOW),
+            vmem((96, 384), LOW),
             vmem((4, 24, 1536), LOW),
             vmem((3, 24, 1536), LOW),
             dma((16,)),
             dma((4,)),
             dma((2,)),
             dma((2,)),
-            dma((2, 6, 1)),
-            dma((2, 6, 3)),
-            dma((2, 5)),
-            dma((5,)),
+            dma((2, 7, 1)),
+            dma((2, 7, 3)),
+            dma((2, 6)),
+            dma((6,)),
             dma((2, 3)),
             dma((2, 2, 3)),
             dma((2, 7)),
@@ -1366,27 +1394,30 @@
     result, full, acts, ffn, us, inv, kv, pc, ps, wst = forward(
         inputs, memory_flat, lengths, norms, shards, images, queries, mem_rows
     )
-    spread, contracted, rest, keys, memory_grad, input_grad, sums = backward(
+    spread, contracted, co, mid, late, last, keys, memory_grad, input_grad, sums = backward(
         norms[::2], padded(cotangent), tokens, memory_flat, (full, acts, ffn, us, inv, kv, pc, ps, wst),
         images, queries, mem_rows,
     )
     share = self_query.shape[0]
     sums = lax.dynamic_slice(sums, (0, lax.axis_index("dp") * share), (8, share))
-    rest = rest.astype(WIDE)
+
+    def beside(halves):
+        return jnp.concatenate([halves[0], halves[1]], axis=1).astype(WIDE)
+
     return (
         cut(result),
         cut(input_grad),
         memory_grad.reshape(memory.shape).astype(WIDE),
-        rest[1, 1],
-        rest[2, 0],
-        rest[2, 1],
-        rest[1, 0],
-        rest[0, 1],
+        late[0].astype(WIDE),
+        beside(last),
+        late[1].astype(WIDE),
+        mid[1].astype(WIDE),
+        mid[0].astype(WIDE),
         keys[:, :width],
         keys[:, width:],
-        rest[0, 0],
-        jnp.concatenate([spread[0], spread[1]], axis=1).astype(WIDE),
-        jnp.concatenate([contracted[0], contracted[1]], axis=1).astype(WIDE),
+        beside(co),
+        beside(spread),
+        beside(contracted),
         *[sums[place] for place in range(6)],
     )
 

time: 223 us -> 216 us (0.969)
  Pallas kernels: 204 us -> 196 us
  other arithmetic: 4.61 us -> 6.96 us
    pallas_call x1, Pallas kernels: 98 us -> 89.5 us  [backward(): pl.pallas_call(functools.partial(backward_kernel, images, queries, mem_ro...]
    convert_element_type x3 -> x5, other arithmetic: 2.36 us -> 4.71 us  [the longest x4 3.68 us: beside(): return jnp.concatenate([halves[0], halves[1]], axis=1).astype(WIDE)]
    unnamed x18 -> x24, local copies, waits for them, and re-layouts: 5.57 us -> 5.69 us
where the time goes in v5:
time: 216 us
  Pallas kernels  196 us (91%)
  local copies, waits for them, and re-layouts  12.4 us (6%)
  other arithmetic  6.96 us (3%)
    pallas_call x1, Pallas kernels, forward(): pl.pallas_call(functools.partial(forward_kernel, images, queries, mem_row...  106 us
    pallas_call x1, Pallas kernels, backward(): pl.pallas_call(functools.partial(backward_kernel, images, queries, mem_ro...  89.5 us
    unnamed x24, local copies, waits for them, and re-layouts  5.69 us

profile of v5, /device:TPU:0, one launch (start us, length us, event | category | flops | bytes accessed | tf_op | source)
XLA Modules:
  0.0 215.7 jit_solution(17774317449572002546)
XLA Ops:
  0.7 2.0 copy.39.refs_0_
  2.6 106.1 %forward.1 = (f32[448,768]{1,0:T(8,128)}, bf16[12288,768]{1,0:T(8,128)(2,1)}, bf16[8,448,768]{2,1,0:T(8,128)(2,1)}, bf16[2,448,3072]{2,1,0:T(8,128)(2,1)}, f32[3...) custom-call(bf16[4,100,768]{2,1,0:T(8,128)(2,1)} %copy.39.refs_0_, ...), custom_call_target="tpu_custom_call" | custom-call | tf_op jit(solution)/shard_map/forward/pallas_call | solution.py:746
  108.7 1.4 slice.88
  110.1 0.0 copy-start.2
  110.1 1.5 copy.44
  111.7 0.1 copy.46
  111.7 0.9 pad.7.clone
  112.6 0.3 copy-done
  112.9 0.9 pad.8.clone
  113.8 89.5 %backward.1 = (bf16[2,96,1536]{2,1,0:T(8,128)(2,1)}, bf16[2,384,384]{2,1,0:T(8,128)(2,1)}, bf16[2,96,384]{2,1,0:T(8,128)(2,1)}, bf16[2,96,768]{2,1,0:T(8,128)(2,...) custom-call(f32[768]{0:T(1024)} %refs_0_.2, ...), custom_call_target="tpu_custom_call" | custom-call | tf_op jit(solution)/shard_map/backward/pallas_call | solution.py:1286
  203.3 1.4 slice.89
  204.7 1.5 copy.45
  206.2 0.2 copy-done.1
  206.4 2.3 %convert.5 = f32[4,320,768]{2,1,0:T(8,128)} convert(bf16[4,320,768]{2,1,0:T(8,128)(2,1)S(1)} %bitcast.51) | non-fusion elementwise | flops 983040 | bytes 5898240 | tf_op jit(solution)/shard_map/convert_element_type | solution.py:1410
  208.7 1.0 bitcast_convert_fusion
  209.8 0.1 copy-done.9
  209.9 0.7 maximum_convert_fusion.2
  210.6 0.7 fusion
  211.3 0.7 maximum_convert_fusion.3
  212.1 1.1 maximum_convert_fusion
  213.2 0.1 slice_bitcast_fusion.1
  213.3 1.1 maximum_convert_fusion.1
  214.4 0.8 constant_dynamic-slice_fusion
  215.1 0.5 slice_bitcast_fusion.8
  (18 shorter events, 0.1 us)
Async XLA Ops:
  110.1 1.5 copy-start.2
  111.7 1.2 copy-start
  204.7 1.8 copy-start.1
  206.4 2.3 %copy-start.5 = (bf16[2,96,768]{2,1,0:T(8,128)(2,1)S(1)}, bf16[2,96,768]{2,1,0:T(8,128)(2,1)}, u32[]{:S(2)}) copy-start(bf16[2,96,768]{2,1,0:T(8,128)(2,1)} %get-tuple-element.53) | copy-start | bytes 884740
  206.4 2.3 %copy-start.6 = (bf16[2,96,768]{2,1,0:T(8,128)(2,1)S(1)}, bf16[2,96,768]{2,1,0:T(8,128)(2,1)}, u32[]{:S(2)}) copy-start(bf16[2,96,768]{2,1,0:T(8,128)(2,1)} %get-tuple-element.51) | copy-start | bytes 884740
  208.7 1.1 copy-start.8
  208.7 1.2 copy-start.9
  208.7 1.9 copy-start.7
  209.8 2.3 %copy-start.4 = (bf16[2,96,1536]{2,1,0:T(8,128)(2,1)S(1)}, bf16[2,96,1536]{2,1,0:T(8,128)(2,1)}, u32[]{:S(2)}) copy-start(bf16[2,96,1536]{2,1,0:T(8,128)(2,1)} %get-tuple-element.56) | copy-start | bytes 1769476
  212.1 1.2 copy-start.3
